TPU v7x, 256 devices: a whole 4x4x8 slice. The times are simulated.
256 devices in a mesh: rows: 16 (over z, core), cols: 16 (over y, x).
Axes of the slice: x: 4, y: 4, z: 8, core: 2. Of those that a mesh axis runs over, the one named last changes fastest.
Arguments:
- in_flight: bfloat16 [16, 2, 16, 128, 16, 128], P('rows', None, 'cols'), may hold values from -0.11 to 1.36
- top_boundary: bfloat16 [2, 16, 128, 16, 128], P(None, 'cols'), may hold values from -0.11 to 1.36
- peps: bfloat16 [16, 16, 4, 4, 4, 4, 2], P('rows', 'cols'), may hold values from -0.21 to 1.46
- sketch: bfloat16 [16, 2, 16, 128, 16, 128], P('rows', None, 'cols'), may hold values from -0.11 to 1.36
Outputs:
- boundary_out: float32 [16, 2, 16, 128, 16, 128], P('rows', None, 'cols')
All inputs are finite; a program needn't handle non-finite values.
Results may differ from a plain program's by a relative error of at most 0.011.
Values may be sent and summed in bfloat16 or wider, within the bound.
No kernel may reach another device: no remote copies, remote signals or barrier semaphores. Data moves between devices by JAX's collectives and lax.ppermute only.
A program may use at most 128 MiB of HBM per device.

v0:
```python
import jax
import jax.numpy as jnp
from jax import lax
from jax.sharding import PartitionSpec as P


def shifted(x, axis, by):
    count = lax.axis_size(axis)
    return lax.ppermute(x, axis, [(i, (i + by) % count) for i in range(count)])


def shifted_2(value, axis, steps):
    count = lax.axis_size(axis)
    first, last = (max(0, -steps), min(count, count - steps))
    return lax.ppermute(value, axis, [(source, source + steps) for source in range(first, last)])


def site_image(tensor_in, right_sketch, left_sketch, site_peps):
    bond_keep = tensor_in.shape[0]
    doubled = tensor_in.shape[1]
    peps_bond = site_peps.shape[0]
    crossed = jnp.dot(
        tensor_in.reshape(bond_keep * doubled, bond_keep),
        right_sketch.reshape(bond_keep, doubled * bond_keep),
        preferred_element_type=jnp.float32,
    ).astype(jnp.bfloat16)
    crossed = crossed.reshape(bond_keep, peps_bond, peps_bond, peps_bond, peps_bond, bond_keep)
    ket_side = jnp.einsum(
        "auvrsb,lurdp->avsldpb", crossed, site_peps, preferred_element_type=jnp.float32
    ).astype(jnp.bfloat16)
    layered = jnp.einsum(
        "avsldpb,mvsep->almdeb", ket_side, site_peps, preferred_element_type=jnp.float32
    ).astype(jnp.bfloat16)
    image = jnp.dot(
        left_sketch.reshape(bond_keep * doubled, bond_keep).T,
        layered.reshape(bond_keep * doubled, doubled * bond_keep),
        preferred_element_type=jnp.float32,
    )
    return image.reshape(bond_keep, doubled, bond_keep)


def factorize(matrix, bond_keep, doubled):
    gram = jnp.dot(
        matrix.T, matrix, precision=lax.Precision.HIGHEST, preferred_element_type=jnp.float32
    ) / (bond_keep * doubled)
    lower = jnp.linalg.cholesky(gram)
    factor = jax.scipy.linalg.solve_triangular(lower, matrix.T, lower=True).T
    carried = lower.T / jnp.sqrt(bond_keep * jnp.mean(lower * lower) + 1e-06)
    return (factor, carried)


def advance_block(carried, images, closing):
    columns, bond_keep, doubled = (images.shape[0], images.shape[1], images.shape[2])
    matrix = jnp.dot(
        carried,
        images[0].reshape(bond_keep, doubled * bond_keep),
        precision=lax.Precision.HIGHEST,
        preferred_element_type=jnp.float32,
    ).reshape(bond_keep * doubled, bond_keep)
    factor, carried = factorize(matrix, bond_keep, doubled)
    factor = jnp.where(closing, matrix, factor)
    results = [factor.reshape(bond_keep, doubled, bond_keep)]
    return (carried, jnp.stack(results))


def on_device(in_flight, top_boundary, peps, sketch):
    members = in_flight.shape[1]
    columns = in_flight.shape[2]
    bond_keep = in_flight.shape[3]
    row_place = lax.axis_index("rows")
    col_place = lax.axis_index("cols")
    col_count = lax.axis_size("cols")
    closing = col_place == col_count - 1
    identity = jnp.eye(bond_keep, dtype=jnp.float32)
    left_edge = shifted(sketch[0, :, columns - 1], "cols", 1)
    arrived = shifted_2(in_flight[0], "rows", 1)
    incoming = jnp.where(row_place == 0, top_boundary, arrived)
    image_list = []
    for member in range(members):
        boundary_now = incoming[member]
        left_sketch = left_edge[member]
        member_images = [site_image(boundary_now[0], sketch[0, member, 0], left_sketch, peps[0, 0])]
        image_list.append(jnp.stack(member_images))
    images = jnp.stack(image_list)
    empty_block = jnp.zeros(images.shape[1:], jnp.float32)
    blocks = []
    for member in range(members):

        def turn(moment, state, member=member):
            outgoing, block = state
            received = shifted_2(outgoing, "cols", 1)
            start = jnp.where(col_place == 0, identity, received)

            def active(unused):
                return advance_block(start, images[member], closing)

            def resting(unused):
                return (outgoing, block)

            return lax.cond(col_place == moment, active, resting, 0)

        _, block = lax.fori_loop(0, col_count, turn, (identity, empty_block))
        blocks.append(block)
    result = jnp.stack(blocks)
    return result[None]


def solution(mesh):
    return jax.shard_map(
        on_device,
        mesh=mesh,
        in_specs=(
            P("rows", None, "cols", None, None, None),
            P(None, "cols", None, None, None),
            P("rows", "cols", None, None, None, None, None),
            P("rows", None, "cols", None, None, None),
        ),
        out_specs=P("rows", None, "cols", None, None, None),
        check_vma=False,
    )
```

profile of v0, /device:TPU:158, one launch (start us, length us, event | category | flops | bytes accessed | tf_op | source)
XLA Modules:
  0.0 1147.9 jit_solution(17847038693891560638)
XLA Ops:
  4.6 12.9 %collective-permute-done.2 = bf16[2,1,128,16,128]{4,3,2,1,0:T(8,128)(2,1)S(1)} collective-permute-done((bf16[2,1,128,16,128]{4,3,2,1,0:T(8,128)(2,1)}, bf16[2,1,128,16,128]{4,3,2,1,0:T(8,128)(2,1)S(1)}, u32[]{:S(2)}, u32[]{:S(2)}) %collective-permute-start.2) | collective-permute-done | bytes 1048608 | tf_op jit(solution)/shard_map/ppermute | solution.py:15
  17.8 5.6 convolution_convert_fusion.1
  23.4 14.5 %reshape.36 = bf16[128,4,4,4,4,128,1,1]{5,4,3,2,1,0,6,7:T(4,128)(2,1)} reshape(bf16[2048,2048]{1,0:T(8,128)(2,1)} %convolution_convert_fusion.1) | data formatting | bytes 16777216 | tf_op jit(solution)/shard_map/reshape | solution.py:27
  37.9 15.3 %fusion.30 = bf16[128,4,4,128,4,4,2,1]{3,5,7,6,4,2,1,0:T(4,128)(2,1)S(1)} fusion(bf16[128,4,4,4,4,128,1,1]{5,4,3,2,1,0,6,7:T(4,128)(2,1)} %reshape.36, bf16[4,4,4,4,2,1,1,1]{3,4,2,1,0,5,6,7:T(2,128)(2,1)S(1)} %bitcast.140), kind=kOutput, calls=%fused_computation.54 | convolution fusion | flops 268435456 | bytes 25166848 | tf_op jit(solution)/shard_map/auvrsb,lurdp->avsldpb/dot_general | solution.py:28
  53.2 16.6 %fusion.26 = bf16[128,4,4,4,4,128]{5,4,2,3,1,0:T(4,128)(2,1)} fusion(bf16[4,4,4,4,2,1,1,1]{1,3,2,4,0,7,6,5:T(4,128)(2,1)S(1)} %copy.41, bf16[128,4,4,128,4,4,2,1]{3,5,7,6,4,2,1,0:T(4,128)(2,1)S(1)} %fusion.30), kind=kOutput, calls=%fused_computation.50 | convolution fusion | flops 272629760 | bytes 25166848 | tf_op jit(solution)/shard_map/avsldpb,mvsep->almdeb/dot_general | solution.py:31
  69.8 8.3 copy.30
  78.1 14.5 %reshape.33 = bf16[2048,2048]{1,0:T(8,128)(2,1)} reshape(bf16[128,4,4,4,4,128]{5,4,3,2,1,0:T(4,128)(2,1)} %copy.30) | data formatting | bytes 16777216 | tf_op jit(solution)/shard_map/reshape | solution.py:36
  94.8 5.8 convolution_bitcast_fusion.3
  102.0 5.6 convolution_convert_fusion
  107.5 14.3 %reshape.42 = bf16[128,4,4,4,4,128,1,1]{5,4,3,2,1,0,6,7:T(4,128)(2,1)} reshape(bf16[2048,2048]{1,0:T(8,128)(2,1)} %convolution_convert_fusion) | data formatting | bytes 16777216 | tf_op jit(solution)/shard_map/reshape | solution.py:27
  121.9 15.5 %fusion.28 = bf16[128,4,4,128,4,4,2,1]{3,5,7,6,4,2,1,0:T(4,128)(2,1)S(1)} fusion(bf16[128,4,4,4,4,128,1,1]{5,4,3,2,1,0,6,7:T(4,128)(2,1)} %reshape.42, bf16[4,4,4,4,2,1,1,1]{3,4,2,1,0,5,6,7:T(2,128)(2,1)S(1)} %bitcast.141), kind=kOutput, calls=%fused_computation.52 | convolution fusion | flops 268435456 | bytes 25166848 | tf_op jit(solution)/shard_map/auvrsb,lurdp->avsldpb/dot_general | solution.py:28
  137.3 16.6 %fusion.27 = bf16[128,4,4,4,4,128]{5,4,2,3,1,0:T(4,128)(2,1)} fusion(bf16[4,4,4,4,2,1,1,1]{1,3,2,4,0,7,6,5:T(4,128)(2,1)S(1)} %copy.41, bf16[128,4,4,128,4,4,2,1]{3,5,7,6,4,2,1,0:T(4,128)(2,1)S(1)} %fusion.28), kind=kOutput, calls=%fused_computation.51 | convolution fusion | flops 272629760 | bytes 25166848 | tf_op jit(solution)/shard_map/avsldpb,mvsep->almdeb/dot_general | solution.py:31
  154.0 8.3 copy.33
  162.3 14.6 %reshape.35 = bf16[2048,2048]{1,0:T(8,128)(2,1)} reshape(bf16[128,4,4,4,4,128]{5,4,3,2,1,0:T(4,128)(2,1)} %copy.33) | data formatting | bytes 16777216 | tf_op jit(solution)/shard_map/reshape | solution.py:36
  176.9 5.8 convolution_bitcast_fusion.2
  185.1 595.1 %while.34 = (s32[]{:T(128)}, f32[128,128]{0,1:T(8,128)S(1)}, f32[1,128,16,128]{3,2,1,0:T(8,128)}, s32[]{:T(128)}, pred[]{:T(512)}, /*index=5*/f32[128,2048]{1,0:T(8,128)}, pred[]{:T(512)}, s32[]{:T(128)}) while((s32[]{:T(128)}, f32[128,128]{0,1:T(8,128)S(1)}, f32[1,128,16,128]{3,2,1,0:T(8,128)}, s32[]{:T(128)}, pred[]{:T(512)}, ...), condition=%wide.region_6.9_spmd.clone, body=%wide.region_0.8_spmd.clone.sunk | while | flops 1208533120 | bytes 13960456 | solution.py:102
  186.9 4.8 collective-permute-done
  193.1 5.1 collective-permute-done
  199.6 4.9 collective-permute-done
  212.1 5.4 collective-permute-done
  219.0 6.7 collective-permute-done
  227.1 7.0 collective-permute-done
  235.5 6.8 collective-permute-done
  243.8 6.9 collective-permute-done
  252.1 6.9 collective-permute-done
  260.5 7.3 collective-permute-done
  269.2 7.4 collective-permute-done
  278.0 6.7 collective-permute-done
  286.1 6.6 collective-permute-done
  294.1 6.9 collective-permute-done
  302.5 445.8 %collective-permute-done = f32[128,128]{1,0:T(8,128)S(1)} collective-permute-done((f32[128,128]{1,0:T(8,128)S(1)}, f32[128,128]{1,0:T(8,128)S(1)}, u32[]{:S(2)}, u32[]{:S(2)}) %collective-permute-start) | collective-permute-done | bytes 65568 | tf_op jit(solution)/shard_map/while/body/eval_jaxpr/ppermute | solution.py:15
  748.2 31.9 %conditional.6 = ((f32[128,128]{0,1:T(8,128)S(1)}, f32[1,128,16,128]{3,2,1,0:T(8,128)})) conditional(s32[]{:T(128)} %convert_element_type.104, (f32[128,128]{0,1:T(8,128)S(1)}, f32[1,128,16,128]{3,2,1,0:T(8,128)}) %tuple.97, (pred[]{:T(512)}, f32[128,128]{1,0:T(8,128)S(1)}, f32[128,128]{1,0:T(8,128)S(1)}, f32[128,2048]{1,0:T(8,128)}, pred[]{:T(512)}) %tuple.98), branch_computations={%region_1.1_spmd, %region_2.7_spmd} | conditional | flops 1208500352 | bytes 13501509 | solution.py:100
  752.6 11.7 %cholesky.44 = f32[128,128]{1,0:T(8,128)S(1)} custom-call(f32[128,128]{1,0:T(8,128)S(1)} %fusion.7), custom_call_target="Cholesky" | custom-call | tf_op jit(solution)/shard_map/while/body/eval_jaxpr/cond/branch_1_fun/jit(cholesky)/cholesky | solution.py:46
  767.6 9.8 custom-call.6
  780.2 364.8 %while.35 = (s32[]{:T(128)}, f32[128,128]{0,1:T(8,128)S(1)}, f32[1,128,16,128]{3,2,1,0:T(8,128)S(1)}, s32[]{:T(128)}, pred[]{:T(512)}, /*index=5*/f32[128,2048]{1,0:T(8,128)}, pred[]{:T(512)}, s32[]{:T(128)}) while((s32[]{:T(128)}, f32[128,128]{0,1:T(8,128)S(1)}, f32[1,128,16,128]{3,2,1,0:T(8,128)S(1)}, s32[]{:T(128)}, ...), condition=%wide.region_11.14_spmd.clone, body=%wide.region_7.0_spmd.clone.sunk | while | flops 1208533120 | bytes 13960456 | solution.py:102
  800.6 5.2 collective-permute-done.1
  807.2 5.4 collective-permute-done.1
  814.0 5.5 collective-permute-done.1
  820.9 5.0 collective-permute-done.1
  846.1 6.9 collective-permute-done.1
  854.4 6.9 collective-permute-done.1
  862.8 6.9 collective-permute-done.1
  871.1 6.9 collective-permute-done.1
  879.5 6.9 collective-permute-done.1
  887.9 226.2 %collective-permute-done.1 = f32[128,128]{1,0:T(8,128)S(1)} collective-permute-done((f32[128,128]{1,0:T(8,128)S(1)}, f32[128,128]{1,0:T(8,128)S(1)}, u32[]{:S(2)}, u32[]{:S(2)}) %collective-permute-start.1) | collective-permute-done | bytes 65568 | tf_op jit(solution)/shard_map/while/body/eval_jaxpr/ppermute | solution.py:15
  1114.1 30.9 %conditional.7 = ((f32[128,128]{0,1:T(8,128)S(1)}, f32[1,128,16,128]{3,2,1,0:T(8,128)S(1)})) conditional(s32[]{:T(128)} %convert_element_type.106, (f32[128,128]{0,1:T(8,128)S(1)}, f32[1,128,16,128]{3,2,1,0:T(8,128)S(1)}) %tuple.100, (pred[]{:T(512)}, f32[128,128]{1,0:T(8,128)S(1)}, f32[128,128]{1,0:T(8,128)S(1)}, f32[128,2048]{1,0:T(8,128)}, ...), branch_computations={%region_8.10_spmd, %region_9.12_spmd} | conditional | flops 1208500352 | bytes 13501509 | solution.py:100
  1118.4 11.7 %cholesky.55 = f32[128,128]{1,0:T(8,128)S(1)} custom-call(f32[128,128]{1,0:T(8,128)S(1)} %fusion.14), custom_call_target="Cholesky" | custom-call | tf_op jit(solution)/shard_map/while/body/eval_jaxpr/cond/branch_1_fun/jit(cholesky)/cholesky | solution.py:46
  1133.5 9.8 custom-call.7
  (181 shorter events, 110.1 us)
Async XLA Ops:
  0.0 17.5 %collective-permute-start.2 = (bf16[2,1,128,16,128]{4,3,2,1,0:T(8,128)(2,1)}, bf16[2,1,128,16,128]{4,3,2,1,0:T(8,128)(2,1)S(1)}, u32[]{:S(2)}, u32[]{:S(2)}) collective-permute-start(bf16[2,1,128,16,128]{4,3,2,1,0:T(8,128)(2,1)} %bitcast.142), channel_id=1, source_target_pairs={{0,16},{16,32},{32,48},{48,64},{64,80},{80,96},{96,112},{112,128},... | collective-permute-start | bytes 3145736 | tf_op jit(solution)/shard_map/ppermute | solution.py:15
  1.9 90.8 %collective-permute-start.3 = (bf16[2,128,16,128]{3,2,1,0:T(8,128)(2,1)}, bf16[2,128,16,128]{3,2,1,0:T(8,128)(2,1)}, u32[]{:S(2)}, u32[]{:S(2)}) collective-permute-start(bf16[2,128,16,128]{3,2,1,0:T(8,128)(2,1)} %bitcast.136), channel_id=1, source_target_pairs={{0,1},{1,2},{2,3},{3,4},{4,5},{5,6},{6,7},{7,8},{8,9},{9,10},{10,1... | collective-permute-start | bytes 3145736 | tf_op jit(solution)/shard_map/ppermute | solution.py:9
  2.1 21.2 %copy-start = (f32[128,128]{0,1:T(8,128)}, f32[128,128]{0,1:T(8,128)S(1)}, u32[]{:S(2)}) copy-start(f32[128,128]{0,1:T(8,128)S(1)} %fusion.40) | copy-start | bytes 196612
  23.4 14.5 %copy-start.4 = (bf16[1,1,4,4,4,4,2]{5,6,4,3,2,1,0:T(2,128)(2,1)S(1)}, bf16[1,1,4,4,4,4,2]{5,6,4,3,2,1,0:T(2,128)(2,1)}, u32[]{:S(2)}) copy-start(bf16[1,1,4,4,4,4,2]{5,6,4,3,2,1,0:T(2,128)(2,1)} %param.17) | copy-start | bytes 3076
  162.3 14.6 %copy-start.3 = (bf16[1,128,16,128]{3,2,1,0:T(8,128)(2,1)S(1)}, bf16[1,128,16,128]{3,2,1,0:T(8,128)(2,1)}, u32[]{:S(2)}) copy-start(bf16[1,128,16,128]{3,2,1,0:T(8,128)(2,1)} %get-tuple-element.478) | copy-start | bytes 1572868
  176.9 8.1 copy-start.2
  185.0 595.2 %copy-start.1 = (f32[128,128]{0,1:T(8,128)S(1)}, f32[128,128]{0,1:T(8,128)}, u32[]{:S(2)}) copy-start(f32[128,128]{0,1:T(8,128)} %copy-done) | copy-start | bytes 196612
  185.5 6.2 collective-permute-start
  191.8 6.4 collective-permute-start
  198.3 6.2 collective-permute-start
  204.6 6.2 collective-permute-start
  210.8 6.7 collective-permute-start
  217.6 8.1 collective-permute-start
  225.8 8.3 collective-permute-start
  234.2 8.1 collective-permute-start
  242.4 8.3 collective-permute-start
  250.8 8.3 collective-permute-start
  259.2 8.7 collective-permute-start
  267.9 8.7 collective-permute-start
  276.7 8.0 collective-permute-start
  284.8 7.9 collective-permute-start
  292.8 8.3 collective-permute-start
  301.2 447.1 %collective-permute-start = (f32[128,128]{1,0:T(8,128)S(1)}, f32[128,128]{1,0:T(8,128)S(1)}, u32[]{:S(2)}, u32[]{:S(2)}) collective-permute-start(f32[128,128]{1,0:T(8,128)S(1)} %copy.84), channel_id=1, source_target_pairs={{0,1},{1,2},{2,3},{3,4},{4,5},{5,6},{6,7},{7,8},{8,9},{9,10},{10,1... | collective-permute-start | bytes 196616 | tf_op jit(solution)/shard_map/while/body/eval_jaxpr/ppermute | solution.py:15
  780.5 6.2 collective-permute-start.1
  786.8 6.2 collective-permute-start.1
  793.0 6.2 collective-permute-start.1
  799.3 6.5 collective-permute-start.1
  805.9 6.7 collective-permute-start.1
  812.7 6.8 collective-permute-start.1
  819.6 6.3 collective-permute-start.1
  826.0 6.2 collective-permute-start.1
  832.3 6.2 collective-permute-start.1
  838.5 6.2 collective-permute-start.1
  844.8 8.2 collective-permute-start.1
  853.1 8.3 collective-permute-start.1
  861.4 8.3 collective-permute-start.1
  869.8 8.3 collective-permute-start.1
  878.2 8.3 collective-permute-start.1
  886.5 227.6 %collective-permute-start.1 = (f32[128,128]{1,0:T(8,128)S(1)}, f32[128,128]{1,0:T(8,128)S(1)}, u32[]{:S(2)}, u32[]{:S(2)}) collective-permute-start(f32[128,128]{1,0:T(8,128)S(1)} %copy.85), channel_id=1, source_target_pairs={{0,1},{1,2},{2,3},{3,4},{4,5},{5,6},{6,7},{7,8},{8,9},{9,10},{10,1... | collective-permute-start | bytes 196616 | tf_op jit(solution)/shard_map/while/body/eval_jaxpr/ppermute | solution.py:15
where the time goes:
time: 1150 us
  waiting for transfers between devices  864 us (75%)
  matrix products  97 us (8%)
  local copies, waits for them, and re-layouts  88.7 us (8%)
  other arithmetic  51.5 us (4%)
  starting transfers between devices  43.5 us (4%)
    ppermute x33, waiting for transfers between devices, shifted_2(): lax.ppermute(value, axis, [(source, source + steps) for source in range(f...  864 us
    ppermute x33, starting transfers between devices, shifted_2(): lax.ppermute(value, axis, [(source, source + steps) for source in range(f...  43.3 us
    dot_general x2, matrix products, site_image(): jnp.einsum('avsldpb,mvsep->almdeb', ket_side, site_peps, preferred_elemen...  33.3 us
    dot_general x2, matrix products, site_image(): jnp.einsum('auvrsb,lurdp->avsldpb', crossed, site_peps, preferred_element...  30.7 us
    reshape x2, local copies, waits for them, and re-layouts, site_image(): layered.reshape(bond_keep * doubled, doubled * bond_keep)  29.1 us
    reshape x2, local copies, waits for them, and re-layouts, site_image(): crossed.reshape(bond_keep, peps_bond, peps_bond, peps_bond, peps_bond, bo...  28.8 us
    another operation x6, other arithmetic, factorize(): lower = jnp.linalg.cholesky(gram)  24.9 us
  transfers between devices with their start and end apart: 34, of which 33 were waited for; matrix products, arithmetic and copies ran while one was open for 7% of the time, Pallas kernels for 0%

commit v1 on v0

v1 whole, which is shorter than its diff:
```python
import functools
import jax
import jax.numpy as jnp
from jax import lax
from jax.experimental import pallas as pl
from jax.experimental.pallas import tpu as pltpu
from jax.sharding import PartitionSpec as P

F32, BF16 = jnp.float32, jnp.bfloat16
NN = (((1,), (0,)), ((), ()))
NT = (((1,), (1,)), ((), ()))

def mm(a, b, dims=NN):
    return lax.dot_general(a, b, dims, preferred_element_type=F32)

def split(x):
    high = x.astype(BF16)
    return high, (x - high.astype(F32)).astype(BF16)

def mm3(a, b, dims=NN):
    return mm(a[0], b[0], dims) + (mm(a[0], b[1], dims) + mm(a[1], b[0], dims))

def picker(first):
    row = lax.broadcasted_iota(jnp.int32, (256, 16), 0)
    col = lax.broadcasted_iota(jnp.int32, (256, 16), 1)
    i1, i2, i3, i4 = row // 64, (row // 16) % 4, (row // 4) % 4, row % 4
    want = i1 * 4 + i3 if first else i2 * 4 + i4
    return jnp.where(want == col, 1.0, 0.0).astype(BF16)

def image_kernel(place_ref, inc_ref, top_ref, sk_ref, left_ref, site_ref, image_ref, w_ref, crossed_ref, layered_ref, acc_ref):
    one, two = picker(True), picker(False)
    joined = jnp.zeros((256, 256), F32)
    for p in range(site_ref.shape[0]):
        site = site_ref[p]
        ket = mm(mm(one, site).astype(BF16), one, NT)
        bra = mm(mm(two, site).astype(BF16), two, NT)
        joined = joined + ket * bra
    w_ref[...] = joined.astype(BF16)
    acc_ref[...] = jnp.zeros_like(acc_ref)

    def chunk(i, carry):
        rows = pl.ds(pl.multiple_of(i * 256, 256), 256)
        inc = jnp.where(place_ref[3] == 0, top_ref[rows, :], inc_ref[rows, :])
        for n in range(8):
            part = mm(inc, sk_ref[:, 256 * n:256 * n + 256]).astype(BF16)
            crossed_ref[2 * n] = part[:, :128]
            crossed_ref[2 * n + 1] = part[:, 128:]
        w = w_ref[...]
        for a in range(0, 16, 2):
            pair = jnp.concatenate([crossed_ref[:, 16 * q:16 * q + 16, :].reshape(256, 128) for q in (a, a + 1)], axis=1)
            lay = mm(w, pair).astype(BF16)
            for k, q in enumerate((a, a + 1)):
                layered_ref[:, 16 * q:16 * q + 16, :] = lay[:, 128 * k:128 * k + 128].reshape(16, 16, 128)
        left = left_ref[:, rows]
        for n in range(8):
            both = jnp.concatenate([layered_ref[2 * n], layered_ref[2 * n + 1]], axis=1)
            acc_ref[:, 256 * n:256 * n + 256] += mm(left, both)
        return carry

    lax.fori_loop(0, 8, chunk, 0)
    for e in range(16):
        flipped = acc_ref[:, 128 * e:128 * e + 128].T
        high, low = split(flipped)
        image_ref[0, 128 * e:128 * e + 128, :] = high
        image_ref[1, 128 * e:128 * e + 128, :] = low

VM = pl.BlockSpec(memory_space=pltpu.VMEM)
def image_call(place, inc, top, sk, left, site):
    return pl.pallas_call(
        image_kernel,
        out_shape=jax.ShapeDtypeStruct((2, 2048, 128), BF16),
        in_specs=[pl.BlockSpec(memory_space=pltpu.SMEM)] + [VM] * 5,
        out_specs=VM,
        scratch_shapes=[pltpu.VMEM((256, 256), BF16), pltpu.VMEM((16, 256, 128), BF16), pltpu.VMEM((16, 256, 128), BF16), pltpu.VMEM((128, 2048), F32)],
        compiler_params=pltpu.CompilerParams(vmem_limit_bytes=32 << 20),
        cost_estimate=pl.CostEstimate(flops=4 * 10**9, bytes_accessed=3 << 20, transcendentals=0),
        name="image",
    )(place, inc, top, sk, left, site)

def step(x, high, low):
    xs = split(x)
    g = jnp.zeros((128, 128), F32)
    nb = 4
    for q in range(0, 16, nb):
        rows = slice(128 * q, 128 * (q + nb))
        h, l = high[rows, :], low[rows, :]
        z = mm3((h, l), xs)
        zh, zl = split(z)
        def lanes(t):
            return jnp.concatenate([t[128 * i:128 * i + 128] for i in range(nb)], axis=1)
        zh, zl, h, l = lanes(zh), lanes(zl), lanes(h), lanes(l)
        g = g + mm3((zh, zl), (h, l), NT)
    return g * (1.0 / 2048)

def normalized(g):
    eye = lax.broadcasted_iota(jnp.int32, g.shape, 0) == lax.broadcasted_iota(jnp.int32, g.shape, 1)
    trace = jnp.sum(jnp.sum(jnp.where(eye, g, 0.0), axis=1, keepdims=True), axis=0, keepdims=True)
    return g / (trace * (1.0 / 128) + 1e-6)

def eliminate(mats, with_inverse, upper_refs, inv_refs, nb=4):
    n = 128
    tiles = [[m[8 * i:8 * i + 8, :] for i in range(n // 8)] for m in mats]
    lane = lax.broadcasted_iota(jnp.int32, (8, n), 1)
    sub = lax.broadcasted_iota(jnp.int32, (8, n), 0)
    inv = [[jnp.where(lane == sub + 8 * i, 1.0, 0.0) for i in range(n // 8)] if w else None for w in with_inverse]
    for k in range(0, n, nb):
        t = k // 8
        for m in range(len(mats)):
            tile = tiles[m][t]
            rows, cols, erows = [], [], []
            for i in range(nb):
                s = k + i - 8 * t
                rows.append(tile[s:s + 1, :])
                if with_inverse[m]:
                    erows.append(inv[m][t][s:s + 1, :])
            el = {}
            for i in range(nb):
                for j in range(i, nb):
                    el[i, j] = jnp.broadcast_to(rows[i][:, k + j:k + j + 1], (1, n))
            fac = {}; d = []
            for i in range(nb):
                v = el[i, i]
                for q in range(i):
                    v = v - fac[q, i] * fac[q, i]
                d.append(lax.rsqrt(v))
                for j in range(i + 1, nb):
                    v = el[i, j]
                    for q in range(i):
                        v = v - fac[q, i] * fac[q, j]
                    fac[i, j] = v * d[i]
            urows, eurows = [], []
            for i in range(nb):
                v = rows[i]
                for q in range(i):
                    v = v - fac[q, i] * urows[q]
                urows.append(v * d[i])
                if with_inverse[m]:
                    v = erows[i]
                    for q in range(i):
                        v = v - fac[q, i] * eurows[q]
                    eurows.append(v * d[i])
            for i in range(nb):
                keep = lax.broadcasted_iota(jnp.int32, (1, n), 1) >= k + i
                upper_refs[m][k + i:k + i + 1, :] = jnp.where(keep, urows[i], 0.0)
                if with_inverse[m]:
                    inv_refs[m][k + i:k + i + 1, :] = eurows[i]
            first = (k + nb) // 8
            for tt in range(first, n // 8):
                tl = tiles[m][tt]
                cs = []
                for i in range(nb):
                    c = jnp.broadcast_to(tl[:, k + i:k + i + 1], (8, n))
                    for q in range(i):
                        c = c - fac[q, i] * cs[q]
                    cs.append(c * d[i])
                for i in range(nb):
                    tl = tl - cs[i] * urows[i]
                tiles[m][tt] = tl
                if with_inverse[m]:
                    e = inv[m][tt]
                    for i in range(nb):
                        e = e - cs[i] * eurows[i]
                    inv[m][tt] = e


def chain_kernel(turn, place_ref, x_ref, own0, own1, a01, a02, a03, a11, a12, a13, kept_in, send_ref, kept_ref, buf, gbuf, in_sem, out_sem):
    x_place, y_place, core = place_ref[0], place_ref[1], place_ref[2]
    sources = ((own0, a01, a02, a03), (own1, a11, a12, a13))

    @pl.when((y_place == turn) & (x_place // 2 == core))
    def _():
        for m in range(2):
            @pl.when(x_place % 2 == m)
            def _():
                for o in range(4):
                    slot = (x_place + o) % 4
                    pltpu.make_async_copy(sources[m][o], buf.at[slot], in_sem.at[slot]).start()
        g = x_ref[...]
        gbuf[0] = g
        copies = [pltpu.make_async_copy(gbuf.at[0], kept_ref.at[0], out_sem.at[0])]
        copies[0].start()
        for i in range(4):
            x = identity() if turn == 0 and i == 0 else normalized(g)
            pltpu.make_async_copy(own0, buf.at[i], in_sem.at[i]).wait()
            g = step(x, buf.at[i, 0], buf.at[i, 1])
            gbuf[i + 1] = g
            copies.append(pltpu.make_async_copy(gbuf.at[i + 1], kept_ref.at[i + 1], out_sem.at[i + 1]))
            copies[-1].start()
        send_ref[...] = g
        for copy in copies:
            copy.wait()


def identity():
    row = lax.broadcasted_iota(jnp.int32, (128, 128), 0)
    return jnp.where(row == lax.broadcasted_iota(jnp.int32, (128, 128), 1), 1.0, 0.0)


def chain_call(turn, place, x, own, arrived, kept):
    any_spec = pl.BlockSpec(memory_space=pl.ANY)
    return pl.pallas_call(
        functools.partial(chain_kernel, turn),
        out_shape=[jax.ShapeDtypeStruct((128, 128), F32), jax.ShapeDtypeStruct((5, 128, 128), F32)],
        in_specs=[pl.BlockSpec(memory_space=pltpu.SMEM), VM] + [any_spec] * 9,
        out_specs=[VM, any_spec],
        scratch_shapes=[
            pltpu.VMEM((4, 2, 2048, 128), BF16), pltpu.VMEM((5, 128, 128), F32),
            pltpu.SemaphoreType.DMA((4,)), pltpu.SemaphoreType.DMA((5,)),
        ],
        input_output_aliases={10: 1},
        compiler_params=pltpu.CompilerParams(vmem_limit_bytes=24 << 20),
        name="chain",
    )(place, x, *own, *arrived[0], *arrived[1], kept)


def final_kernel(place_ref, image0, image1, kept_ref, r1, r2, r3, out_ref, upper_ref, inverse_ref, m_ref):
    x_place, y_place, core = place_ref[0], place_ref[1], place_ref[2]
    first = (x_place == 0) & (y_place == 0)
    closing = (x_place == 3) & (y_place == 3)
    left, here = [], []
    for m in range(2):
        offset = (x_place + 8 - 2 * core - m) % 4
        pair = []
        for q in range(2):
            g = kept_ref[x_place + q]
            for o, r in enumerate((r1, r2, r3)):
                g = jnp.where(offset == o + 1, r[q], g)
            pair.append(g)
        left.append(jnp.where(first, identity(), normalized(pair[0])))
        here.append(pair[1])
    eliminate(left + here, [False, False, True, True], [upper_ref.at[i] for i in range(4)], [None, None, inverse_ref.at[0], inverse_ref.at[1]])
    for m, image in enumerate((image0, image1)):
        r = split(upper_ref[m])
        inverse = split(inverse_ref[m])
        for e in range(0, 16, 2):
            rows = slice(128 * e, 128 * e + 256)
            both = mm3(r, (image[0, rows, :], image[1, rows, :]), NT)
            for k in range(2):
                matrix = both[:, 128 * k:128 * k + 128]
                factor = mm3(split(matrix), inverse, NT)
                out_ref[0, m, 0, :, e + k, :] = jnp.where(closing, matrix, factor)


def final_call(place, images, kept, returned):
    return pl.pallas_call(
        final_kernel,
        out_shape=jax.ShapeDtypeStruct((1, 2, 1, 128, 16, 128), F32),
        in_specs=[pl.BlockSpec(memory_space=pltpu.SMEM)] + [VM] * 6,
        out_specs=VM,
        scratch_shapes=[pltpu.VMEM((4, 128, 128), F32), pltpu.VMEM((2, 128, 128), F32), pltpu.VMEM((8, 128), F32)],
        compiler_params=pltpu.CompilerParams(vmem_limit_bytes=32 << 20),
        name="final",
    )(place, *images, kept, *returned)


def on_device(in_flight, top_boundary, peps, sketch):
    row, col = lax.axis_index("rows"), lax.axis_index("cols")
    rows, cols = lax.axis_size("rows"), lax.axis_size("cols")
    x_place, y_place, core = col % 4, col // 4, row % 2
    place = jnp.stack([x_place, y_place, core, row]).astype(jnp.int32)
    both = ("rows", "cols")
    site = jnp.transpose(peps[0, 0], (4, 3, 0, 2, 1)).reshape(2, 16, 16)
    down = [(i, i + 1) for i in range(rows - 1)]
    right = [(i, (i + 1) % cols) for i in range(cols)]
    own_sketch = sketch[0, :, 0]
    flipped = jnp.swapaxes(own_sketch.reshape(2, 2048, 128), 1, 2)
    images = []
    for m in range(2):
        arrived = lax.ppermute(in_flight[0, m, 0].reshape(2048, 128), "rows", down)
        left = lax.ppermute(flipped[m], "cols", right)
        images.append(image_call(place, arrived, top_boundary[m, 0].reshape(2048, 128), own_sketch[m].reshape(128, 2048), left, site))

    def group(m, offset, outward):
        pairs = []
        for r in range(rows):
            for y in range(4):
                host = 2 * (r % 2) + m
                other = (host + offset) % 4
                a, b = r * cols + 4 * y + host, r * cols + 4 * y + other
                pairs.append((a, b) if outward else (b, a))
        return pairs

    arrivals = [[lax.ppermute(images[m], both, group(m, o, False)) for o in (1, 2, 3)] for m in range(2)]
    kept = jnp.zeros((5, 128, 128), F32)
    x = jnp.zeros((128, 128), F32)
    for turn in range(4):
        sent, kept = chain_call(turn, place, x, images, arrivals, kept)
        if turn < 3:
            pairs = [(r * cols + 4 * turn + 2 * (r % 2) + m, r * cols + 4 * turn + 4 + 2 * (r % 2) + m) for r in range(rows) for m in range(2)]
            x = lax.ppermute(sent, both, pairs)
    returned = []
    for o in (1, 2, 3):
        mine = lax.dynamic_slice(kept, ((x_place + o) % 4, 0, 0), (2, 128, 128))
        returned.append(lax.ppermute(mine, both, group(0, o, True) + group(1, o, True)))
    return final_call(place, images, kept, returned)


def solution(mesh):
    return jax.shard_map(
        on_device,
        mesh=mesh,
        in_specs=(
            P("rows", None, "cols", None, None, None),
            P(None, "cols", None, None, None),
            P("rows", "cols", None, None, None, None, None),
            P("rows", None, "cols", None, None, None),
        ),
        out_specs=P("rows", None, "cols", None, None, None),
        check_vma=False,
    )
```

time: 1150 us -> 169 us (0.15)
  the two profiles are of different devices: /device:TPU:158 before, /device:TPU:248 now
where the time goes in v1:
time: 169 us; the launch traced here: 168 us
  waiting for transfers between devices  60.4 us (36%)
  starting transfers between devices  47.6 us (28%)
  Pallas kernels  46.4 us (27%)
  local copies, waits for them, and re-layouts  13.1 us (8%)
    ppermute x3, waiting for transfers between devices, on_device(): x = lax.ppermute(sent, both, pairs)  28.2 us
    ppermute x6, starting transfers between devices, on_device(): lax.ppermute(images[m], both, group(m, o, False))  20.2 us
    pallas_call x2, Pallas kernels, image_call(): pl.pallas_call(image_kernel, out_shape=jax.ShapeDtypeStruct((2, 2048, 128...  19.6 us
    pallas_call x1, Pallas kernels, final_call(): pl.pallas_call(final_kernel, out_shape=jax.ShapeDtypeStruct((1, 2, 1, 128...  16.7 us
    ppermute x3, starting transfers between devices, on_device(): lax.ppermute(mine, both, group(0, o, True) + group(1, o, True))  16.5 us
    ppermute x2, waiting for transfers between devices, on_device(): left = lax.ppermute(flipped[m], 'cols', right)  15.4 us
    ppermute x6, waiting for transfers between devices, on_device(): lax.ppermute(images[m], both, group(m, o, False))  12.2 us
    pallas_call x4, Pallas kernels, chain_call(): pl.pallas_call(functools.partial(chain_kernel, turn), out_shape=[jax.Shap...  10 us
  transfers between devices with their start and end apart: 16, of which 6 were waited for; matrix products, arithmetic and copies ran while one was open for 3% of the time, Pallas kernels for 6%

profile of v1, /device:TPU:248, one launch (start us, length us, event | category | flops | bytes accessed | tf_op | source)
XLA Modules:
  0.0 168.0 jit_solution(12374731706050383241)
XLA Ops:
  0.0 1.6 copy.11
  1.6 0.0 copy-start.10
  1.6 1.0 slice_bitcast_fusion
  2.6 1.5 collective-permute-start.1
  4.1 1.1 fusion.2
  5.3 2.0 %collective-permute-start = (bf16[2048,128]{1,0:T(8,128)(2,1)}, bf16[2048,128]{1,0:T(8,128)(2,1)S(1)}, u32[]{:S(2)}, u32[]{:S(2)}) collective-permute-start(bf16[2048,128]{1,0:T(8,128)(2,1)} %bitcast.4), channel_id=1, source_target_pairs={{0,16},{16,32},{32,48},{48,64},{64,80},{80,96},{96,112},{112,128},... | collective-permute-start | bytes 1572872 | tf_op jit(solution)/shard_map/ppermute | solution.py:269
  7.4 1.0 fusion
  8.4 0.1 copy.18
  8.5 0.3 copy.12
  8.8 0.1 reshape.7.site_ref
  8.9 0.1 pad_add_fusion.place_ref
  9.0 1.4 fusion.1
  10.4 8.2 %collective-permute-done.1.left_ref = bf16[128,2048]{1,0:T(8,128)(2,1)S(1)} collective-permute-done((bf16[128,2048]{1,0:T(8,128)(2,1)}, bf16[128,2048]{1,0:T(8,128)(2,1)S(1)}, u32[]{:S(2)}, u32[]{:S(2)}) %collective-permute-start.1) | collective-permute-done | bytes 524320 | tf_op jit(solution)/shard_map/ppermute | solution.py:270
  18.6 9.8 %image.2.own0.image0 = bf16[2,2048,128]{2,1,0:T(8,128)(2,1)S(1)} custom-call(s32[4]{0:T(128)S(1)} %pad_add_fusion.place_ref, bf16[2048,128]{1,0:T(8,128)(2,1)S(1)} %collective-permute-done.inc_ref, bf16[2048,128]{1,0:T(8,128)(2,1)S(1)} %bitcast.30, bf16[128,2048]{1,0:T(8,128)(2,1)S(1)} %bitcast.27, bf16[128,2048]{1,0:T(8,128)(2,1)S(1)} %collective-permute-done.1.left_ref, ...), custom_call_target="tpu_custom_call" | custom-call | flops 4000000000 | bytes 3145728 | tf_op jit(solution)/shard_map/image/pallas_call | solution.py:69
  28.5 1.3 collective-permute-start.4
  29.8 2.8 %collective-permute-start.3 = (bf16[128,2048]{1,0:T(8,128)(2,1)S(1)}, bf16[128,2048]{1,0:T(8,128)(2,1)S(1)}, u32[]{:S(2)}, u32[]{:S(2)}) collective-permute-start(bf16[128,2048]{1,0:T(8,128)(2,1)S(1)} %copy-done.13), channel_id=1, source_target_pairs={{0,1},{1,2},{2,3},{3,4},{4,5},{5,6},{6,7},{7,8},{8,9},{9,10},{10,1... | collective-permute-start | bytes 1572872 | tf_op jit(solution)/shard_map/ppermute | solution.py:270
  32.5 1.9 %collective-permute-start.2 = (bf16[2048,128]{1,0:T(8,128)(2,1)S(1)}, bf16[2048,128]{1,0:T(8,128)(2,1)S(1)}, u32[]{:S(2)}, u32[]{:S(2)}) collective-permute-start(bf16[2048,128]{1,0:T(8,128)(2,1)S(1)} %bitcast.35), channel_id=1, source_target_pairs={{0,16},{16,32},{32,48},{48,64},{64,80},{80,96},{96,112},{112,128},... | collective-permute-start | bytes 1572872 | tf_op jit(solution)/shard_map/ppermute | solution.py:269
  34.5 0.1 copy.17
  34.6 1.3 collective-permute-start.5
  35.9 1.3 collective-permute-start.6
  37.2 7.1 %collective-permute-done.3.left_ref = bf16[128,2048]{1,0:T(8,128)(2,1)S(1)} collective-permute-done((bf16[128,2048]{1,0:T(8,128)(2,1)S(1)}, bf16[128,2048]{1,0:T(8,128)(2,1)S(1)}, u32[]{:S(2)}, u32[]{:S(2)}) %collective-permute-start.3) | collective-permute-done | bytes 524320 | tf_op jit(solution)/shard_map/ppermute | solution.py:270
  44.4 0.0 collective-permute-done.2.inc_ref
  44.4 9.8 %image.3.own1.image1 = bf16[2,2048,128]{2,1,0:T(8,128)(2,1)S(1)} custom-call(s32[4]{0:T(128)S(1)} %pad_add_fusion.place_ref, bf16[2048,128]{1,0:T(8,128)(2,1)S(1)} %collective-permute-done.2.inc_ref, bf16[2048,128]{1,0:T(8,128)(2,1)S(1)} %bitcast.29, bf16[128,2048]{1,0:T(8,128)(2,1)S(1)} %bitcast.28, bf16[128,2048]{1,0:T(8,128)(2,1)S(1)} %collective-permute-done.3.left_ref, ...), custom_call_target="tpu_custom_call" | custom-call | flops 4000000000 | bytes 3145728 | tf_op jit(solution)/shard_map/image/pallas_call | solution.py:69
  54.2 0.7 collective-permute-start.7
  54.9 0.7 collective-permute-start.8
  55.6 0.0 collective-permute-done.4.a01
  55.7 14.9 %collective-permute-start.9 = (bf16[2,2048,128]{2,1,0:T(8,128)(2,1)S(1)}, bf16[2,2048,128]{2,1,0:T(8,128)(2,1)S(1)}, u32[]{:S(2)}, u32[]{:S(2)}) collective-permute-start(bf16[2,2048,128]{2,1,0:T(8,128)(2,1)S(1)} %image.3.own1.image1), channel_id=1, source_target_pairs={{0,1},{4,5},{8,9},{12,13},{18,19},{22,23},{26,27},{30,31},{32,33},... | collective-permute-start | bytes 3145736 | tf_op jit(solution)/shard_map/ppermute | solution.py:283
  70.6 0.0 copy-start
  70.7 12.1 %collective-permute-done.9.a13 = bf16[2,2048,128]{2,1,0:T(8,128)(2,1)S(1)} collective-permute-done((bf16[2,2048,128]{2,1,0:T(8,128)(2,1)S(1)}, bf16[2,2048,128]{2,1,0:T(8,128)(2,1)S(1)}, u32[]{:S(2)}, u32[]{:S(2)}) %collective-permute-start.9) | collective-permute-done | bytes 1048608 | tf_op jit(solution)/shard_map/ppermute | solution.py:283
  82.8 0.6 chain.4
  83.5 0.7 collective-permute-start.10
  84.2 0.9 chain.5
  85.0 0.7 collective-permute-start.11
  85.8 1.3 chain.6
  87.0 1.3 collective-permute-start.12
  88.4 28.2 %collective-permute-done.12.x_ref = f32[128,128]{1,0:T(8,128)S(1)} collective-permute-done((f32[128,128]{1,0:T(8,128)}, f32[128,128]{1,0:T(8,128)S(1)}, u32[]{:S(2)}, u32[]{:S(2)}) %collective-permute-start.12) | collective-permute-done | bytes 65568 | tf_op jit(solution)/shard_map/ppermute | solution.py:290
  116.6 1.2 copy-done.1
  117.9 1.2 copy-done.3
  119.1 1.2 copy-done.5
  120.3 1.2 copy-done.7
  121.5 1.2 copy-done.9
  122.8 7.3 %chain.7 = (f32[128,128]{1,0:T(8,128)}, f32[5,128,128]{2,1,0:T(8,128)S(1)}) custom-call(s32[4]{0:T(128)S(1)} %pad_add_fusion.place_ref, f32[128,128]{1,0:T(8,128)S(1)} %collective-permute-done.12.x_ref, bf16[2,2048,128]{2,1,0:T(8,128)(2,1)S(1)} %image.2.own0.image0, bf16[2,2048,128]{2,1,0:T(8,128)(2,1)S(1)} %image.3.own1.image1, ...), custom_call_target="tpu_custom_call", output_to_operand_aliasing={{1}: (10, {})} | custom-call | tf_op jit(solution)/shard_map/chain/pallas_call | solution.py:201
  130.1 13.0 %collective-permute-start.13 = (f32[2,128,128]{2,1,0:T(8,128)S(1)}, f32[2,128,128]{2,1,0:T(8,128)S(1)}, u32[]{:S(2)}, u32[]{:S(2)}) collective-permute-start(f32[2,128,128]{2,1,0:T(8,128)S(1)} %get-tuple-element.29), channel_id=1, source_target_pairs={{0,1},{4,5},{8,9},{12,13},{18,19},{22,23},{26,27},{30,31},{32,33},... | collective-permute-start | bytes 393224 | tf_op jit(solution)/shard_map/ppermute | solution.py:294
  143.1 1.3 collective-permute-start.14
  144.4 2.2 %collective-permute-start.15 = (f32[2,128,128]{2,1,0:T(8,128)S(1)}, f32[2,128,128]{2,1,0:T(8,128)S(1)}, u32[]{:S(2)}, u32[]{:S(2)}) collective-permute-start(f32[2,128,128]{2,1,0:T(8,128)S(1)} %get-tuple-element.27), channel_id=1, source_target_pairs={{0,3},{4,7},{8,11},{12,15},{18,17},{22,21},{26,25},{30,29},{32,35}... | collective-permute-start | bytes 393224 | tf_op jit(solution)/shard_map/ppermute | solution.py:294
  146.6 0.4 collective-permute-done.14.r2
  147.0 4.3 %collective-permute-done.15.r3 = f32[2,128,128]{2,1,0:T(8,128)S(1)} collective-permute-done((f32[2,128,128]{2,1,0:T(8,128)S(1)}, f32[2,128,128]{2,1,0:T(8,128)S(1)}, u32[]{:S(2)}, u32[]{:S(2)}) %collective-permute-start.15) | collective-permute-done | bytes 131104 | tf_op jit(solution)/shard_map/ppermute | solution.py:294
  151.3 16.7 %final.1 = f32[1,2,1,128,16,128]{5,4,3,2,1,0:T(8,128)} custom-call(s32[4]{0:T(128)S(1)} %pad_add_fusion.place_ref, bf16[2,2048,128]{2,1,0:T(8,128)(2,1)S(1)} %image.2.own0.image0, bf16[2,2048,128]{2,1,0:T(8,128)(2,1)S(1)} %image.3.own1.image1, f32[5,128,128]{2,1,0:T(8,128)S(1)} %get-tuple-element.18.kept_ref, f32[2,128,128]{2,1,0:T(8,128)S(1)} %collective-permute-done.13.r1, ...), custom_call_target="tpu_custom_call" | custom-call | tf_op jit(solution)/shard_map/final/pallas_call | solution.py:245
  (36 shorter events, 0.1 us)
Async XLA Ops:
  0.0 4.1 %copy-start.12 = (bf16[1,2,1,128,16,128]{5,4,3,2,1,0:T(8,128)(2,1)S(1)}, bf16[1,2,1,128,16,128]{5,4,3,2,1,0:T(8,128)(2,1)}, u32[]{:S(2)}) copy-start(bf16[1,2,1,128,16,128]{5,4,3,2,1,0:T(8,128)(2,1)} %param.4) | copy-start | bytes 3145732
  1.6 5.8 %copy-start.10 = (bf16[1,2,1,128,16,128]{5,4,3,2,1,0:T(8,128)(2,1)S(1)}, bf16[1,2,1,128,16,128]{5,4,3,2,1,0:T(8,128)(2,1)}, u32[]{:S(2)}) copy-start(bf16[1,2,1,128,16,128]{5,4,3,2,1,0:T(8,128)(2,1)} %param.7) | copy-start | bytes 3145732
  2.6 16.0 %collective-permute-start.1 = (bf16[128,2048]{1,0:T(8,128)(2,1)}, bf16[128,2048]{1,0:T(8,128)(2,1)S(1)}, u32[]{:S(2)}, u32[]{:S(2)}) collective-permute-start(bf16[128,2048]{1,0:T(8,128)(2,1)} %get-tuple-element.20), channel_id=1, source_target_pairs={{0,1},{1,2},{2,3},{3,4},{4,5},{5,6},{6,7},{7,8},{8,9},{9,10},{10,1... | collective-permute-start | bytes 1572872 | tf_op jit(solution)/shard_map/ppermute | solution.py:270
  5.3 3.2 %copy-start.15 = (bf16[1,1,4,4,4,4,2]{5,6,4,3,2,1,0:T(2,128)(2,1)S(1)}, bf16[1,1,4,4,4,4,2]{5,6,4,3,2,1,0:T(2,128)(2,1)}, u32[]{:S(2)}) copy-start(bf16[1,1,4,4,4,4,2]{5,6,4,3,2,1,0:T(2,128)(2,1)} %param.6) | copy-start | bytes 3076
  5.3 13.3 %collective-permute-start = (bf16[2048,128]{1,0:T(8,128)(2,1)}, bf16[2048,128]{1,0:T(8,128)(2,1)S(1)}, u32[]{:S(2)}, u32[]{:S(2)}) collective-permute-start(bf16[2048,128]{1,0:T(8,128)(2,1)} %bitcast.4), channel_id=1, source_target_pairs={{0,16},{16,32},{32,48},{48,64},{64,80},{80,96},{96,112},{112,128},... | collective-permute-start | bytes 1572872 | tf_op jit(solution)/shard_map/ppermute | solution.py:269
  18.6 11.1 %copy-start.13 = (bf16[128,2048]{1,0:T(8,128)(2,1)S(1)}, bf16[128,2048]{1,0:T(8,128)(2,1)}, u32[]{:S(2)}) copy-start(bf16[128,2048]{1,0:T(8,128)(2,1)} %get-tuple-element.19) | copy-start | bytes 1572868
  18.6 13.9 %copy-start.14 = (bf16[1,1,1,128,16,128]{5,4,3,2,1,0:T(8,128)(2,1)S(1)}, bf16[1,1,1,128,16,128]{5,4,3,2,1,0:T(8,128)(2,1)}, u32[]{:S(2)}) copy-start(bf16[1,1,1,128,16,128]{5,4,3,2,1,0:T(8,128)(2,1)} %get-tuple-element.25) | copy-start | bytes 1572868
  18.6 15.8 %copy-start.11 = (bf16[1,1,1,128,16,128]{5,4,3,2,1,0:T(8,128)(2,1)S(1)}, bf16[1,1,1,128,16,128]{5,4,3,2,1,0:T(8,128)(2,1)}, u32[]{:S(2)}) copy-start(bf16[1,1,1,128,16,128]{5,4,3,2,1,0:T(8,128)(2,1)} %get-tuple-element.21) | copy-start | bytes 1572868
  28.5 27.2 %collective-permute-start.4 = (bf16[2,2048,128]{2,1,0:T(8,128)(2,1)S(1)}, bf16[2,2048,128]{2,1,0:T(8,128)(2,1)S(1)}, u32[]{:S(2)}, u32[]{:S(2)}) collective-permute-start(bf16[2,2048,128]{2,1,0:T(8,128)(2,1)S(1)} %image.2.own0.image0), channel_id=1, source_target_pairs={{1,0},{5,4},{9,8},{13,12},{19,18},{23,22},{27,26},{31,30},{33,32},... | collective-permute-start | bytes 3145736 | tf_op jit(solution)/shard_map/ppermute | solution.py:283
  29.8 14.6 %collective-permute-start.3 = (bf16[128,2048]{1,0:T(8,128)(2,1)S(1)}, bf16[128,2048]{1,0:T(8,128)(2,1)S(1)}, u32[]{:S(2)}, u32[]{:S(2)}) collective-permute-start(bf16[128,2048]{1,0:T(8,128)(2,1)S(1)} %copy-done.13), channel_id=1, source_target_pairs={{0,1},{1,2},{2,3},{3,4},{4,5},{5,6},{6,7},{7,8},{8,9},{9,10},{10,1... | collective-permute-start | bytes 1572872 | tf_op jit(solution)/shard_map/ppermute | solution.py:270
  32.5 11.8 %collective-permute-start.2 = (bf16[2048,128]{1,0:T(8,128)(2,1)S(1)}, bf16[2048,128]{1,0:T(8,128)(2,1)S(1)}, u32[]{:S(2)}, u32[]{:S(2)}) collective-permute-start(bf16[2048,128]{1,0:T(8,128)(2,1)S(1)} %bitcast.35), channel_id=1, source_target_pairs={{0,16},{16,32},{32,48},{48,64},{64,80},{80,96},{96,112},{112,128},... | collective-permute-start | bytes 1572872 | tf_op jit(solution)/shard_map/ppermute | solution.py:269
  34.6 35.9 %collective-permute-start.5 = (bf16[2,2048,128]{2,1,0:T(8,128)(2,1)S(1)}, bf16[2,2048,128]{2,1,0:T(8,128)(2,1)S(1)}, u32[]{:S(2)}, u32[]{:S(2)}) collective-permute-start(bf16[2,2048,128]{2,1,0:T(8,128)(2,1)S(1)} %image.2.own0.image0), channel_id=1, source_target_pairs={{2,0},{6,4},{10,8},{14,12},{16,18},{20,22},{24,26},{28,30},{34,32}... | collective-permute-start | bytes 3145736 | tf_op jit(solution)/shard_map/ppermute | solution.py:283
  35.9 34.7 %collective-permute-start.6 = (bf16[2,2048,128]{2,1,0:T(8,128)(2,1)S(1)}, bf16[2,2048,128]{2,1,0:T(8,128)(2,1)S(1)}, u32[]{:S(2)}, u32[]{:S(2)}) collective-permute-start(bf16[2,2048,128]{2,1,0:T(8,128)(2,1)S(1)} %image.2.own0.image0), channel_id=1, source_target_pairs={{3,0},{7,4},{11,8},{15,12},{17,18},{21,22},{25,26},{29,30},{35,32}... | collective-permute-start | bytes 3145736 | tf_op jit(solution)/shard_map/ppermute | solution.py:283
  54.2 16.4 %collective-permute-start.7 = (bf16[2,2048,128]{2,1,0:T(8,128)(2,1)S(1)}, bf16[2,2048,128]{2,1,0:T(8,128)(2,1)S(1)}, u32[]{:S(2)}, u32[]{:S(2)}) collective-permute-start(bf16[2,2048,128]{2,1,0:T(8,128)(2,1)S(1)} %image.3.own1.image1), channel_id=1, source_target_pairs={{2,1},{6,5},{10,9},{14,13},{16,19},{20,23},{24,27},{28,31},{34,33}... | collective-permute-start | bytes 3145736 | tf_op jit(solution)/shard_map/ppermute | solution.py:283
  54.9 15.7 %collective-permute-start.8 = (bf16[2,2048,128]{2,1,0:T(8,128)(2,1)S(1)}, bf16[2,2048,128]{2,1,0:T(8,128)(2,1)S(1)}, u32[]{:S(2)}, u32[]{:S(2)}) collective-permute-start(bf16[2,2048,128]{2,1,0:T(8,128)(2,1)S(1)} %image.3.own1.image1), channel_id=1, source_target_pairs={{3,1},{7,5},{11,9},{15,13},{17,19},{21,23},{25,27},{29,31},{35,33}... | collective-permute-start | bytes 3145736 | tf_op jit(solution)/shard_map/ppermute | solution.py:283
  55.7 27.1 %collective-permute-start.9 = (bf16[2,2048,128]{2,1,0:T(8,128)(2,1)S(1)}, bf16[2,2048,128]{2,1,0:T(8,128)(2,1)S(1)}, u32[]{:S(2)}, u32[]{:S(2)}) collective-permute-start(bf16[2,2048,128]{2,1,0:T(8,128)(2,1)S(1)} %image.3.own1.image1), channel_id=1, source_target_pairs={{0,1},{4,5},{8,9},{12,13},{18,19},{22,23},{26,27},{30,31},{32,33},... | collective-permute-start | bytes 3145736 | tf_op jit(solution)/shard_map/ppermute | solution.py:283
  70.6 15.1 %copy-start = (bf16[2,2048,128]{2,1,0:T(8,128)(2,1)}, bf16[2,2048,128]{2,1,0:T(8,128)(2,1)S(1)}, u32[]{:S(2)}) copy-start(bf16[2,2048,128]{2,1,0:T(8,128)(2,1)S(1)} %collective-permute-done.5.a02) | copy-start | bytes 3145732
  70.6 15.1 %copy-start.2 = (bf16[2,2048,128]{2,1,0:T(8,128)(2,1)}, bf16[2,2048,128]{2,1,0:T(8,128)(2,1)S(1)}, u32[]{:S(2)}) copy-start(bf16[2,2048,128]{2,1,0:T(8,128)(2,1)S(1)} %collective-permute-done.6.a03) | copy-start | bytes 3145732
  70.6 15.1 %copy-start.4 = (bf16[2,2048,128]{2,1,0:T(8,128)(2,1)}, bf16[2,2048,128]{2,1,0:T(8,128)(2,1)S(1)}, u32[]{:S(2)}) copy-start(bf16[2,2048,128]{2,1,0:T(8,128)(2,1)S(1)} %collective-permute-done.7.a11) | copy-start | bytes 3145732
  70.6 15.1 %copy-start.6 = (bf16[2,2048,128]{2,1,0:T(8,128)(2,1)}, bf16[2,2048,128]{2,1,0:T(8,128)(2,1)S(1)}, u32[]{:S(2)}) copy-start(bf16[2,2048,128]{2,1,0:T(8,128)(2,1)S(1)} %collective-permute-done.8.a12) | copy-start | bytes 3145732
  82.8 3.0 %copy-start.8 = (bf16[2,2048,128]{2,1,0:T(8,128)(2,1)}, bf16[2,2048,128]{2,1,0:T(8,128)(2,1)S(1)}, u32[]{:S(2)}) copy-start(bf16[2,2048,128]{2,1,0:T(8,128)(2,1)S(1)} %collective-permute-done.9.a13) | copy-start | bytes 3145732
  83.5 0.7 collective-permute-start.10
  85.0 0.7 collective-permute-start.11
  87.0 29.6 %collective-permute-start.12 = (f32[128,128]{1,0:T(8,128)}, f32[128,128]{1,0:T(8,128)S(1)}, u32[]{:S(2)}, u32[]{:S(2)}) collective-permute-start(f32[128,128]{1,0:T(8,128)} %get-tuple-element.16), channel_id=1, source_target_pairs={{8,12},{9,13},{26,30},{27,31},{40,44},{41,45},{58,62},{59,63},{72,... | collective-permute-start | bytes 196616 | tf_op jit(solution)/shard_map/ppermute | solution.py:290
  116.6 1.2 copy-start.1
  117.9 1.2 copy-start.3
  119.1 1.2 copy-start.5
  120.3 1.2 copy-start.7
  121.5 1.2 copy-start.9
  130.1 16.5 %collective-permute-start.13 = (f32[2,128,128]{2,1,0:T(8,128)S(1)}, f32[2,128,128]{2,1,0:T(8,128)S(1)}, u32[]{:S(2)}, u32[]{:S(2)}) collective-permute-start(f32[2,128,128]{2,1,0:T(8,128)S(1)} %get-tuple-element.29), channel_id=1, source_target_pairs={{0,1},{4,5},{8,9},{12,13},{18,19},{22,23},{26,27},{30,31},{32,33},... | collective-permute-start | bytes 393224 | tf_op jit(solution)/shard_map/ppermute | solution.py:294
  143.1 3.9 %collective-permute-start.14 = (f32[2,128,128]{2,1,0:T(8,128)S(1)}, f32[2,128,128]{2,1,0:T(8,128)S(1)}, u32[]{:S(2)}, u32[]{:S(2)}) collective-permute-start(f32[2,128,128]{2,1,0:T(8,128)S(1)} %get-tuple-element.28), channel_id=1, source_target_pairs={{0,2},{4,6},{8,10},{12,14},{18,16},{22,20},{26,24},{30,28},{32,34}... | collective-permute-start | bytes 393224 | tf_op jit(solution)/shard_map/ppermute | solution.py:294
  144.4 6.9 %collective-permute-start.15 = (f32[2,128,128]{2,1,0:T(8,128)S(1)}, f32[2,128,128]{2,1,0:T(8,128)S(1)}, u32[]{:S(2)}, u32[]{:S(2)}) collective-permute-start(f32[2,128,128]{2,1,0:T(8,128)S(1)} %get-tuple-element.27), channel_id=1, source_target_pairs={{0,3},{4,7},{8,11},{12,15},{18,17},{22,21},{26,25},{30,29},{32,35}... | collective-permute-start | bytes 393224 | tf_op jit(solution)/shard_map/ppermute | solution.py:294

commit v2 on v1

v2 whole, which is shorter than its diff:
```python
import functools
import jax
import jax.numpy as jnp
from jax import lax
from jax.experimental import pallas as pl
from jax.experimental.pallas import tpu as pltpu
from jax.sharding import PartitionSpec as P

F32, BF16 = jnp.float32, jnp.bfloat16
NN = (((1,), (0,)), ((), ()))
NT = (((1,), (1,)), ((), ()))

def mm(a, b, dims=NN):
    return lax.dot_general(a, b, dims, preferred_element_type=F32)

def split(x):
    high = x.astype(BF16)
    return high, (x - high.astype(F32)).astype(BF16)

def mm3(a, b, dims=NN):
    return mm(a[0], b[0], dims) + (mm(a[0], b[1], dims) + mm(a[1], b[0], dims))

def picker(first):
    row = lax.broadcasted_iota(jnp.int32, (256, 16), 0)
    col = lax.broadcasted_iota(jnp.int32, (256, 16), 1)
    i1, i2, i3, i4 = row // 64, (row // 16) % 4, (row // 4) % 4, row % 4
    want = i1 * 4 + i3 if first else i2 * 4 + i4
    return jnp.where(want == col, 1.0, 0.0).astype(BF16)

ROWS = 512


def layered_kernel(place_ref, inc_ref, top_ref, sk_ref, site_ref, layered_ref, w_ref, crossed_ref):
    one, two = picker(True), picker(False)
    joined = jnp.zeros((256, 256), F32)
    for p in range(site_ref.shape[0]):
        site = site_ref[p]
        ket = mm(mm(one, site).astype(BF16), one, NT)
        bra = mm(mm(two, site).astype(BF16), two, NT)
        joined = joined + ket * bra
    w_ref[...] = joined.astype(BF16)
    for m in range(2):
        def chunk(i, carry, m=m):
            start = pl.multiple_of(i * ROWS, ROWS)
            rows = pl.ds(start, ROWS)
            inc = jnp.where(place_ref[3] == 0, top_ref[m, rows, :], inc_ref[m, rows, :])
            for n in range(8):
                part = mm(inc, sk_ref[m, :, 256 * n:256 * n + 256]).astype(BF16)
                crossed_ref[2 * n] = part[:, :128]
                crossed_ref[2 * n + 1] = part[:, 128:]
            w = w_ref[...]
            for a in range(0, ROWS // 16, 2):
                pair = jnp.concatenate([crossed_ref[:, 16 * q:16 * q + 16, :].reshape(256, 128) for q in (a, a + 1)], axis=1)
                lay = mm(w, pair).astype(BF16)
                for k in range(2):
                    layered_ref[m, :, pl.ds(start + 16 * (a + k), 16), :] = lay[:, 128 * k:128 * k + 128].reshape(16, 16, 128)
            return carry

        lax.fori_loop(0, 2048 // ROWS, chunk, 0)


def image_kernel(layered_ref, left_ref, image0_ref, image1_ref):
    for m, image_ref in enumerate((image0_ref, image1_ref)):
        left = left_ref[m].T
        for n in range(0, 16, 2):
            wide = mm(left, cat(layered_ref[m, n], layered_ref[m, n + 1], 1))
            for e in range(2):
                high, low = split(wide[:, 128 * e:128 * e + 128].T)
                rows = slice(128 * (n + e), 128 * (n + e) + 128)
                image_ref[0, rows, :] = high
                image_ref[1, rows, :] = low


VM = pl.BlockSpec(memory_space=pltpu.VMEM)
SCALARS = pl.BlockSpec(memory_space=pltpu.SMEM)


def layered_call(place, inc, top, sk, site):
    return pl.pallas_call(
        layered_kernel,
        out_shape=jax.ShapeDtypeStruct((2, 16, 2048, 128), BF16),
        in_specs=[SCALARS] + [VM] * 4,
        out_specs=VM,
        scratch_shapes=[pltpu.VMEM((256, 256), BF16), pltpu.VMEM((16, ROWS, 128), BF16)],
        compiler_params=pltpu.CompilerParams(vmem_limit_bytes=8 << 20),
        cost_estimate=pl.CostEstimate(flops=1000, bytes_accessed=1000, transcendentals=0),
        name="layered",
    )(place, inc, top, sk, site)


def image_call(layered, left):
    return pl.pallas_call(
        image_kernel,
        out_shape=[jax.ShapeDtypeStruct((2, 2048, 128), BF16)] * 2,
        in_specs=[VM] * 2,
        out_specs=[VM] * 2,
        compiler_params=pltpu.CompilerParams(vmem_limit_bytes=8 << 20),
        cost_estimate=pl.CostEstimate(flops=1000, bytes_accessed=1000, transcendentals=0),
        name="image",
    )(layered, left)


def cat(a, b, axis):
    return jnp.concatenate([a, b], axis=axis)


def lanes(t):
    return jnp.concatenate([t[128 * i:128 * i + 128] for i in range(t.shape[0] // 128)], axis=1)


def step(x, image):
    xh, xl = split(x)
    w = cat(xh, xl, 1)
    h, l = image[0], image[1]
    z = mm(cat(h, l, 1), cat(w, w, 0))
    zh, zl = split(z[:, :128] + z[:, 128:])
    g = mm(cat(lanes(zh), lanes(zl), 0), cat(lanes(h), lanes(l), 0), NT)
    return (g[:128, :128] + (g[:128, 128:] + g[128:, :128]) + g[128:, 128:]) * (1.0 / 2048)


def normalized(g):
    eye = lax.broadcasted_iota(jnp.int32, g.shape, 0) == lax.broadcasted_iota(jnp.int32, g.shape, 1)
    trace = jnp.sum(jnp.sum(jnp.where(eye, g, 0.0), axis=1, keepdims=True), axis=0, keepdims=True)
    return g / (trace * (1.0 / 128) + 1e-6)

def eliminate(mats, with_inverse, upper_refs, inv_refs, nb=4):
    n = 128
    tiles = [[m[8 * i:8 * i + 8, :] for i in range(n // 8)] for m in mats]
    lane = lax.broadcasted_iota(jnp.int32, (8, n), 1)
    sub = lax.broadcasted_iota(jnp.int32, (8, n), 0)
    inv = [[jnp.where(lane == sub + 8 * i, 1.0, 0.0) for i in range(n // 8)] if w else None for w in with_inverse]
    for k in range(0, n, nb):
        t = k // 8
        for m in range(len(mats)):
            tile = tiles[m][t]
            rows, cols, erows = [], [], []
            for i in range(nb):
                s = k + i - 8 * t
                rows.append(tile[s:s + 1, :])
                if with_inverse[m]:
                    erows.append(inv[m][t][s:s + 1, :])
            el = {}
            for i in range(nb):
                for j in range(i, nb):
                    el[i, j] = jnp.broadcast_to(rows[i][:, k + j:k + j + 1], (1, n))
            fac = {}; d = []
            for i in range(nb):
                v = el[i, i]
                for q in range(i):
                    v = v - fac[q, i] * fac[q, i]
                d.append(lax.rsqrt(v))
                for j in range(i + 1, nb):
                    v = el[i, j]
                    for q in range(i):
                        v = v - fac[q, i] * fac[q, j]
                    fac[i, j] = v * d[i]
            urows, eurows = [], []
            for i in range(nb):
                v = rows[i]
                for q in range(i):
                    v = v - fac[q, i] * urows[q]
                urows.append(v * d[i])
                if with_inverse[m]:
                    v = erows[i]
                    for q in range(i):
                        v = v - fac[q, i] * eurows[q]
                    eurows.append(v * d[i])
            for i in range(nb):
                keep = lax.broadcasted_iota(jnp.int32, (1, n), 1) >= k + i
                upper_refs[m][k + i:k + i + 1, :] = jnp.where(keep, urows[i], 0.0)
                if with_inverse[m]:
                    inv_refs[m][k + i:k + i + 1, :] = eurows[i]
            first = (k + nb) // 8
            for tt in range(first, n // 8):
                tl = tiles[m][tt]
                cs = []
                for i in range(nb):
                    c = jnp.broadcast_to(tl[:, k + i:k + i + 1], (8, n))
                    for q in range(i):
                        c = c - fac[q, i] * cs[q]
                    cs.append(c * d[i])
                for i in range(nb):
                    tl = tl - cs[i] * urows[i]
                tiles[m][tt] = tl
                if with_inverse[m]:
                    e = inv[m][tt]
                    for i in range(nb):
                        e = e - cs[i] * eurows[i]
                    inv[m][tt] = e


ANY = pl.BlockSpec(memory_space=pl.ANY)
SMALL = pl.CostEstimate(flops=1000, bytes_accessed=1000, transcendentals=0)
SQUARE = jax.ShapeDtypeStruct((128, 128), F32)
PAIR = jax.ShapeDtypeStruct((2, 128, 128), F32)
QUAD = jax.ShapeDtypeStruct((2, 2, 128, 128), F32)


def params(mib):
    return pltpu.CompilerParams(vmem_limit_bytes=mib << 20)


def identity():
    row = lax.broadcasted_iota(jnp.int32, (128, 128), 0)
    return jnp.where(row == lax.broadcasted_iota(jnp.int32, (128, 128), 1), 1.0, 0.0)


def single_kernel(turn, place_ref, x_ref, image0, image1, kept_in, *rest):
    sends, kept_ref, sem = rest[:-2], rest[-2], rest[-1]

    @pl.when((place_ref[1] == 0) & (place_ref[0] == turn))
    def _():
        copies = [pltpu.make_async_copy(x_ref, kept_ref.at[0], sem.at[0])]
        copies[0].start()
        for m, image in enumerate((image0, image1)):
            x = identity() if turn == 0 else normalized(x_ref[m])
            g = step(x, image)
            send = sends[0].at[m] if len(sends) == 1 else sends[m]
            send[...] = g
            copies.append(pltpu.make_async_copy(send, kept_ref.at[1, m], sem.at[1 + m]))
            copies[-1].start()
        for copy in copies:
            copy.wait()


def single_call(turn, place, x, images, kept):
    sends = [SQUARE, SQUARE] if turn == 3 else [PAIR]
    return pl.pallas_call(
        functools.partial(single_kernel, turn),
        out_shape=sends + [QUAD],
        in_specs=[SCALARS, VM, VM, VM, ANY],
        out_specs=[VM] * len(sends) + [ANY],
        scratch_shapes=[pltpu.SemaphoreType.DMA((3,))],
        input_output_aliases={4: len(sends)},
        compiler_params=params(16),
        cost_estimate=SMALL,
        name="single",
    )(place, x, *images, kept)


def collect_kernel(place_ref, own0, own1, a01, a02, a03, a11, a12, a13, out_ref, sem):
    x_place, y_place, core = place_ref[0], place_ref[1], place_ref[2]
    sources = ((own0, a01, a02, a03), (own1, a11, a12, a13))

    @pl.when((y_place > 0) & (x_place // 2 == core))
    def _():
        for m in range(2):
            @pl.when(x_place % 2 == m)
            def _():
                for o in range(4):
                    pltpu.make_async_copy(sources[m][o], out_ref.at[(x_place + o) % 4], sem.at[o]).start()
        for o in range(4):
            pltpu.make_async_copy(own0, out_ref.at[o], sem.at[o]).wait()


def collect_call(place, images, arrived):
    return pl.pallas_call(
        collect_kernel,
        out_shape=jax.ShapeDtypeStruct((4, 2, 2048, 128), BF16),
        in_specs=[SCALARS] + [ANY] * 8,
        out_specs=ANY,
        scratch_shapes=[pltpu.SemaphoreType.DMA((4,))],
        compiler_params=params(4),
        cost_estimate=SMALL,
        name="collect",
    )(place, *images, *arrived[0], *arrived[1])


def chain_kernel(turn, place_ref, xa_ref, xb_ref, images, i0, i1, i2, i3, send_ref, r0, r1, r2, r3, gbuf, sem):
    x_place, y_place, core = place_ref[0], place_ref[1], place_ref[2]

    @pl.when((y_place == turn) & (x_place // 2 == core))
    def _():
        g = jnp.where(x_place % 2 == 0, xa_ref[...], xb_ref[...])
        gbuf[0] = g
        for i in range(4):
            if turn < 3 or i < 3:
                g = step(normalized(g), images.at[i])
            gbuf[i + 1] = g
        send_ref[...] = g
        copies = [pltpu.make_async_copy(gbuf.at[pl.ds((x_place + o) % 4, 2)], r, sem.at[o]) for o, r in enumerate((r0, r1, r2, r3))]
        for copy in copies:
            copy.start()
        for copy in copies:
            copy.wait()


def chain_call(turn, place, xa, xb, images, returns):
    return pl.pallas_call(
        functools.partial(chain_kernel, turn),
        out_shape=[SQUARE] + [PAIR] * 4,
        in_specs=[SCALARS, VM, VM, VM] + [ANY] * 4,
        out_specs=[VM] + [ANY] * 4,
        scratch_shapes=[pltpu.VMEM((5, 128, 128), F32), pltpu.SemaphoreType.DMA((4,))],
        input_output_aliases={4: 1, 5: 2, 6: 3, 7: 4},
        compiler_params=params(16),
        cost_estimate=SMALL,
        name="chain",
    )(place, xa, xb, images, *returns)


def final_kernel(place_ref, image0, image1, kept_ref, r0, r1, r2, r3, out_ref, upper_ref, inverse_ref, result, sem):
    x_place, y_place, core = place_ref[0], place_ref[1], place_ref[2]
    first = (x_place == 0) & (y_place == 0)
    closing = (x_place == 3) & (y_place == 3)
    left, here = [], []
    for m in range(2):
        offset = jnp.where(y_place == 0, -1, (x_place + 8 - 2 * core - m) % 4)
        pair = []
        for q in range(2):
            g = kept_ref[q, m]
            for o, r in enumerate((r0, r1, r2, r3)):
                g = jnp.where(offset == o, r[q], g)
            pair.append(g)
        left.append(jnp.where(first, identity(), normalized(pair[0])))
        here.append(pair[1])
    eliminate(left + here, [False, False, True, True], [upper_ref.at[i] for i in range(4)], [None, None, inverse_ref.at[0], inverse_ref.at[1]])
    copies = []
    for m, image in enumerate((image0, image1)):
        rh, rl = split(upper_ref[m])
        vh, vl = split(inverse_ref[m])
        r = cat(rh, rl, 0)
        v = cat(cat(vh, vh, 1), cat(vl, vl, 1), 0)
        for q in range(4):
            rows = slice(512 * q, 512 * q + 512)
            parts = mm(r, cat(image[0, rows, :], image[1, rows, :], 0), NT)
            wide = parts[:128, :512] + (parts[:128, 512:] + parts[128:, :512])
            matrix = jnp.concatenate([wide[:, 128 * i:128 * i + 128] for i in range(4)], axis=0)
            mh, ml = split(matrix)
            f = mm(cat(mh, ml, 1), v, NT)
            f = jnp.where(closing, matrix, f[:, :128] + f[:, 128:])
            for i in range(4):
                e = 4 * q + i
                result[m, e] = f[128 * i:128 * i + 128]
                copies.append(pltpu.make_async_copy(result.at[m, e], out_ref.at[0, m, 0, :, e, :], sem))
                copies[-1].start()
    for copy in copies:
        copy.wait()


def final_call(place, images, kept, returned):
    return pl.pallas_call(
        final_kernel,
        out_shape=jax.ShapeDtypeStruct((1, 2, 1, 128, 16, 128), F32),
        in_specs=[SCALARS] + [VM] * 7,
        out_specs=ANY,
        scratch_shapes=[
            pltpu.VMEM((4, 128, 128), F32), pltpu.VMEM((2, 128, 128), F32),
            pltpu.VMEM((2, 16, 128, 128), F32), pltpu.SemaphoreType.DMA,
        ],
        compiler_params=params(16),
        cost_estimate=SMALL,
        name="final",
    )(place, *images, kept, *returned)


def on_device(in_flight, top_boundary, peps, sketch):
    row, col = lax.axis_index("rows"), lax.axis_index("cols")
    rows, cols = lax.axis_size("rows"), lax.axis_size("cols")
    place = jnp.stack([col % 4, col // 4, row % 2, row]).astype(jnp.int32)
    both = ("rows", "cols")
    site = jnp.transpose(peps[0, 0], (4, 3, 0, 2, 1)).reshape(2, 16, 16)
    down = [(i, i + 1) for i in range(rows - 1)]
    right = [(i, (i + 1) % cols) for i in range(cols)]
    top = top_boundary[:, 0].reshape(2, 2048, 128)
    arrived = lax.ppermute(in_flight.reshape(2, 2048, 128), "rows", down)
    left = lax.ppermute(sketch.reshape(2, 2048, 128), "cols", right)
    layered = layered_call(place, arrived, top, sketch.reshape(2, 128, 2048), site)
    images = image_call(layered, left)

    kept = jnp.zeros((2, 2, 128, 128), F32)
    x = jnp.zeros((2, 128, 128), F32)
    for turn in range(3):
        sent, kept = single_call(turn, place, x, images, kept)
        x = lax.ppermute(sent, both, [(r * cols + turn, r * cols + turn + 1) for r in range(rows)])
    sent0, sent1, kept = single_call(3, place, x, images, kept)
    xa, xb = (lax.ppermute(sent, both, [(r * cols + 3, r * cols + 4 + 2 * (r % 2) + m) for r in range(rows)]) for m, sent in enumerate((sent0, sent1)))

    def group(m, offset, outward):
        pairs = []
        for r in range(rows):
            for y in range(1, 4):
                host = 2 * (r % 2) + m
                other = (host + offset) % 4
                a, b = r * cols + 4 * y + host, r * cols + 4 * y + other
                pairs.append((a, b) if outward else (b, a))
        return pairs

    arrivals = [[lax.ppermute(images[m], both, group(m, o, False)) for o in (1, 2, 3)] for m in range(2)]
    gathered = collect_call(place, images, arrivals)
    returns = [jnp.zeros((2, 128, 128), F32) for _ in range(4)]
    for turn in range(1, 4):
        sent, *returns = chain_call(turn, place, xa, xb, gathered, returns)
        if turn < 3:
            pairs = [(r * cols + 4 * turn + 2 * (r % 2) + m, r * cols + 4 * turn + 4 + 2 * (r % 2) + m) for r in range(rows) for m in range(2)]
            xa = xb = lax.ppermute(sent, both, pairs)
    returned = [returns[0]] + [lax.ppermute(returns[o], both, group(0, o, True) + group(1, o, True)) for o in (1, 2, 3)]
    return final_call(place, images, kept, returned)


def solution(mesh):
    return jax.shard_map(
        on_device,
        mesh=mesh,
        in_specs=(
            P("rows", None, "cols", None, None, None),
            P(None, "cols", None, None, None),
            P("rows", "cols", None, None, None, None, None),
            P("rows", None, "cols", None, None, None),
        ),
        out_specs=P("rows", None, "cols", None, None, None),
        check_vma=False,
    )
```

time: 169 us -> 125 us (0.74)
  the two profiles are of different devices: /device:TPU:248 before, /device:TPU:152 now
where the time goes in v2:
time: 125 us
  waiting for transfers between devices  56.4 us (45%)
  Pallas kernels  36.4 us (29%)
  starting transfers between devices  27.1 us (22%)
  local copies, waits for them, and re-layouts  4.01 us (3%)
    ppermute x6, waiting for transfers between devices, on_device(): lax.ppermute(images[m], both, group(m, o, False))  25.2 us
    ppermute x2, waiting for transfers between devices, on_device(): xa = xb = lax.ppermute(sent, both, pairs)  15.2 us
    pallas_call x1, Pallas kernels, final_call(): pl.pallas_call(final_kernel, out_shape=jax.ShapeDtypeStruct((1, 2, 1, 128...  12.8 us
    pallas_call x1, Pallas kernels, layered_call(): pl.pallas_call(layered_kernel, out_shape=jax.ShapeDtypeStruct((2, 16, 204...  11.8 us
    ppermute x1, waiting for transfers between devices, on_device(): arrived = lax.ppermute(in_flight.reshape(2, 2048, 128), 'rows', down)  11.2 us
    ppermute x6, starting transfers between devices, on_device(): lax.ppermute(images[m], both, group(m, o, False))  10.1 us
    ppermute x3, starting transfers between devices, on_device(): lax.ppermute(returns[o], both, group(0, o, True) + group(1, o, True))  8.22 us
    pallas_call x3, Pallas kernels, chain_call(): pl.pallas_call(functools.partial(chain_kernel, turn), out_shape=[SQUARE]...  5.95 us
  transfers between devices with their start and end apart: 18, of which 7 were waited for; matrix products, arithmetic and copies ran while one was open for 2% of the time, Pallas kernels for 12%

profile of v2, /device:TPU:152, one launch (start us, length us, event | category | flops | bytes accessed | tf_op | source)
XLA Modules:
  0.0 124.5 jit_solution(14848869740954728924)
XLA Ops:
  0.0 1.9 %collective-permute-start = (bf16[2,2048,128]{2,1,0:T(8,128)(2,1)}, bf16[2,2048,128]{2,1,0:T(8,128)(2,1)S(1)}, u32[]{:S(2)}, u32[]{:S(2)}) collective-permute-start(bf16[2,2048,128]{2,1,0:T(8,128)(2,1)} %bitcast.15), channel_id=1, source_target_pairs={{0,16},{16,32},{32,48},{48,64},{64,80},{80,96},{96,112},{112,128},... | collective-permute-start | bytes 3145736 | tf_op jit(solution)/shard_map/ppermute | solution.py:366
  1.9 1.6 %collective-permute-start.1 = (bf16[2,2048,128]{2,1,0:T(8,128)(2,1)}, bf16[2,2048,128]{2,1,0:T(8,128)(2,1)S(1)}, u32[]{:S(2)}, u32[]{:S(2)}) collective-permute-start(bf16[2,2048,128]{2,1,0:T(8,128)(2,1)} %bitcast.13), channel_id=1, source_target_pairs={{0,1},{1,2},{2,3},{3,4},{4,5},{5,6},{6,7},{7,8},{8,9},{9,10},{10,1... | collective-permute-start | bytes 3145736 | tf_op jit(solution)/shard_map/ppermute | solution.py:367
  3.5 1.5 %reshape.13.sk_ref = bf16[2,128,2048]{2,1,0:T(8,128)(2,1)S(1)} reshape(bf16[1,2,1,128,16,128]{5,4,3,2,1,0:T(8,128)(2,1)} %param.7) | data formatting | bytes 2097152 | tf_op jit(solution)/shard_map/reshape | solution.py:368
  5.1 1.1 copy.21
  6.1 0.1 reshape.14.site_ref
  6.2 0.1 pad_add_fusion.place_ref
  6.3 11.2 %collective-permute-done.inc_ref = bf16[2,2048,128]{2,1,0:T(8,128)(2,1)S(1)} collective-permute-done((bf16[2,2048,128]{2,1,0:T(8,128)(2,1)}, bf16[2,2048,128]{2,1,0:T(8,128)(2,1)S(1)}, u32[]{:S(2)}, u32[]{:S(2)}) %collective-permute-start) | collective-permute-done | bytes 1048608 | tf_op jit(solution)/shard_map/ppermute | solution.py:366
  17.5 1.2 copy-done
  18.8 11.8 %layered.1.layered_ref = bf16[2,16,2048,128]{3,2,1,0:T(8,128)(2,1)S(1)} custom-call(s32[4]{0:T(128)S(1)} %pad_add_fusion.place_ref, bf16[2,2048,128]{2,1,0:T(8,128)(2,1)S(1)} %collective-permute-done.inc_ref, bf16[2,2048,128]{2,1,0:T(8,128)(2,1)S(1)} %bitcast.12, bf16[2,128,2048]{2,1,0:T(8,128)(2,1)S(1)} %reshape.13.sk_ref, ...), custom_call_target="tpu_custom_call" | custom-call | flops 1000 | bytes 1000 | tf_op jit(solution)/shard_map/layered/pallas_call | solution.py:79
  30.5 0.0 collective-permute-done.1.left_ref
  30.6 2.7 %image.1 = (bf16[2,2048,128]{2,1,0:T(8,128)(2,1)S(1)}, bf16[2,2048,128]{2,1,0:T(8,128)(2,1)S(1)}) custom-call(bf16[2,16,2048,128]{3,2,1,0:T(8,128)(2,1)S(1)} %layered.1.layered_ref, bf16[2,2048,128]{2,1,0:T(8,128)(2,1)S(1)} %collective-permute-done.1.left_ref), custom_call_target="tpu_custom_call" | custom-call | flops 1000 | bytes 1000 | tf_op jit(solution)/shard_map/image/pallas_call | solution.py:92
  33.2 0.7 collective-permute-start.10
  34.0 0.6 single.4
  34.6 0.7 collective-permute-start.2
  35.3 0.0 collective-permute-done.2.x_ref
  35.3 0.6 single.5
  35.9 0.7 collective-permute-start.3
  36.6 0.0 collective-permute-done.3.x_ref
  36.6 0.6 single.6
  37.1 0.7 collective-permute-start.4
  37.8 0.7 collective-permute-start.11
  38.6 4.6 %collective-permute-start.12 = (bf16[2,2048,128]{2,1,0:T(8,128)(2,1)S(1)}, bf16[2,2048,128]{2,1,0:T(8,128)(2,1)S(1)}, u32[]{:S(2)}, u32[]{:S(2)}) collective-permute-start(bf16[2,2048,128]{2,1,0:T(8,128)(2,1)S(1)} %get-tuple-element.31.image1.own1), channel_id=1, source_target_pairs={{4,5},{8,9},{12,13},{22,23},{26,27},{30,31},{36,37},{40,41},{44,45... | collective-permute-start | bytes 3145736 | tf_op jit(solution)/shard_map/ppermute | solution.py:389
  43.2 1.3 %collective-permute-start.7 = (bf16[2,2048,128]{2,1,0:T(8,128)(2,1)S(1)}, bf16[2,2048,128]{2,1,0:T(8,128)(2,1)S(1)}, u32[]{:S(2)}, u32[]{:S(2)}) collective-permute-start(bf16[2,2048,128]{2,1,0:T(8,128)(2,1)S(1)} %get-tuple-element.30.image0.own0), channel_id=1, source_target_pairs={{5,4},{9,8},{13,12},{23,22},{27,26},{31,30},{37,36},{41,40},{45,44... | collective-permute-start | bytes 3145736 | tf_op jit(solution)/shard_map/ppermute | solution.py:389
  44.5 1.3 %collective-permute-start.8 = (bf16[2,2048,128]{2,1,0:T(8,128)(2,1)S(1)}, bf16[2,2048,128]{2,1,0:T(8,128)(2,1)S(1)}, u32[]{:S(2)}, u32[]{:S(2)}) collective-permute-start(bf16[2,2048,128]{2,1,0:T(8,128)(2,1)S(1)} %get-tuple-element.30.image0.own0), channel_id=1, source_target_pairs={{6,4},{10,8},{14,12},{20,22},{24,26},{28,30},{38,36},{42,40},{46,4... | collective-permute-start | bytes 3145736 | tf_op jit(solution)/shard_map/ppermute | solution.py:389
  45.8 1.5 %collective-permute-start.9 = (bf16[2,2048,128]{2,1,0:T(8,128)(2,1)S(1)}, bf16[2,2048,128]{2,1,0:T(8,128)(2,1)S(1)}, u32[]{:S(2)}, u32[]{:S(2)}) collective-permute-start(bf16[2,2048,128]{2,1,0:T(8,128)(2,1)S(1)} %get-tuple-element.30.image0.own0), channel_id=1, source_target_pairs={{7,4},{11,8},{15,12},{21,22},{25,26},{29,30},{39,36},{43,40},{47,4... | collective-permute-start | bytes 3145736 | tf_op jit(solution)/shard_map/ppermute | solution.py:389
  47.3 0.6 single.7
  47.8 0.0 collective-permute-done.11.a12
  47.9 0.7 collective-permute-start.5
  48.5 15.6 %collective-permute-done.12.a13 = bf16[2,2048,128]{2,1,0:T(8,128)(2,1)S(1)} collective-permute-done((bf16[2,2048,128]{2,1,0:T(8,128)(2,1)S(1)}, bf16[2,2048,128]{2,1,0:T(8,128)(2,1)S(1)}, u32[]{:S(2)}, u32[]{:S(2)}) %collective-permute-start.12) | collective-permute-done | bytes 1048608 | tf_op jit(solution)/shard_map/ppermute | solution.py:389
  64.1 0.7 collective-permute-start.6
  64.8 1.8 %collective-permute-done.8.a02 = bf16[2,2048,128]{2,1,0:T(8,128)(2,1)S(1)} collective-permute-done((bf16[2,2048,128]{2,1,0:T(8,128)(2,1)S(1)}, bf16[2,2048,128]{2,1,0:T(8,128)(2,1)S(1)}, u32[]{:S(2)}, u32[]{:S(2)}) %collective-permute-start.8) | collective-permute-done | bytes 1048608 | tf_op jit(solution)/shard_map/ppermute | solution.py:389
  66.6 7.9 %collective-permute-done.9.a03 = bf16[2,2048,128]{2,1,0:T(8,128)(2,1)S(1)} collective-permute-done((bf16[2,2048,128]{2,1,0:T(8,128)(2,1)S(1)}, bf16[2,2048,128]{2,1,0:T(8,128)(2,1)S(1)}, u32[]{:S(2)}, u32[]{:S(2)}) %collective-permute-start.9) | collective-permute-done | bytes 1048608 | tf_op jit(solution)/shard_map/ppermute | solution.py:389
  74.4 0.9 collect.1.images
  75.4 0.0 collective-permute-done.5.xa_ref
  75.4 0.6 chain.3
  76.0 0.7 collective-permute-start.13
  76.7 0.0 collective-permute-done.13.xa_ref.xb_ref
  76.7 0.6 chain.4
  77.3 1.3 %collective-permute-start.14 = (f32[128,128]{1,0:T(8,128)S(1)}, f32[128,128]{1,0:T(8,128)S(1)}, u32[]{:S(2)}, u32[]{:S(2)}) collective-permute-start(f32[128,128]{1,0:T(8,128)S(1)} %get-tuple-element.46), channel_id=1, source_target_pairs={{8,12},{9,13},{26,30},{27,31},{40,44},{41,45},{58,62},{59,63},{72,... | collective-permute-start | bytes 196616 | tf_op jit(solution)/shard_map/ppermute | solution.py:396
  78.6 15.2 %collective-permute-done.14.xa_ref.xb_ref = f32[128,128]{1,0:T(8,128)S(1)} collective-permute-done((f32[128,128]{1,0:T(8,128)S(1)}, f32[128,128]{1,0:T(8,128)S(1)}, u32[]{:S(2)}, u32[]{:S(2)}) %collective-permute-start.14) | collective-permute-done | bytes 65568 | tf_op jit(solution)/shard_map/ppermute | solution.py:396
  93.8 4.8 %chain.5 = (f32[128,128]{1,0:T(8,128)}, f32[2,128,128]{2,1,0:T(8,128)S(1)}, f32[2,128,128]{2,1,0:T(8,128)S(1)}, f32[2,128,128]{2,1,0:T(8,128)S(1)}, f32[2,128,128]{2,1,0:T(8,128)S(1)}) custom-call(s32[4]{0:T(128)S(1)} %pad_add_fusion.place_ref, ...), custom_call_target="tpu_custom_call", output_to_operand_aliasing={{1}: (4, {}), {2}: (5, {}), {3}: (6, {}), {4}: (7, {})} | custom-call | flops 1000 | bytes 1000 | tf_op jit(solution)/shard_map/chain/pallas_call | solution.py:289
  98.6 4.8 %collective-permute-start.15 = (f32[2,128,128]{2,1,0:T(8,128)S(1)}, f32[2,128,128]{2,1,0:T(8,128)S(1)}, u32[]{:S(2)}, u32[]{:S(2)}) collective-permute-start(f32[2,128,128]{2,1,0:T(8,128)S(1)} %get-tuple-element.52), channel_id=1, source_target_pairs={{4,5},{8,9},{12,13},{22,23},{26,27},{30,31},{36,37},{40,41},{44,45... | collective-permute-start | bytes 393224 | tf_op jit(solution)/shard_map/ppermute | solution.py:397
  103.4 1.3 %collective-permute-start.16 = (f32[2,128,128]{2,1,0:T(8,128)S(1)}, f32[2,128,128]{2,1,0:T(8,128)S(1)}, u32[]{:S(2)}, u32[]{:S(2)}) collective-permute-start(f32[2,128,128]{2,1,0:T(8,128)S(1)} %get-tuple-element.53), channel_id=1, source_target_pairs={{4,6},{8,10},{12,14},{22,20},{26,24},{30,28},{36,38},{40,42},{44,4... | collective-permute-start | bytes 393224 | tf_op jit(solution)/shard_map/ppermute | solution.py:397
  104.7 2.1 %collective-permute-start.17 = (f32[2,128,128]{2,1,0:T(8,128)S(1)}, f32[2,128,128]{2,1,0:T(8,128)S(1)}, u32[]{:S(2)}, u32[]{:S(2)}) collective-permute-start(f32[2,128,128]{2,1,0:T(8,128)S(1)} %get-tuple-element.54), channel_id=1, source_target_pairs={{4,7},{8,11},{12,15},{22,21},{26,25},{30,29},{36,39},{40,43},{44,4... | collective-permute-start | bytes 393224 | tf_op jit(solution)/shard_map/ppermute | solution.py:397
  106.8 0.0 collective-permute-done.15.r1
  106.8 0.4 collective-permute-done.16.r2
  107.3 4.3 %collective-permute-done.17.r3 = f32[2,128,128]{2,1,0:T(8,128)S(1)} collective-permute-done((f32[2,128,128]{2,1,0:T(8,128)S(1)}, f32[2,128,128]{2,1,0:T(8,128)S(1)}, u32[]{:S(2)}, u32[]{:S(2)}) %collective-permute-start.17) | collective-permute-done | bytes 131104 | tf_op jit(solution)/shard_map/ppermute | solution.py:397
  111.6 12.8 %final.1 = f32[1,2,1,128,16,128]{5,4,3,2,1,0:T(8,128)} custom-call(s32[4]{0:T(128)S(1)} %pad_add_fusion.place_ref, bf16[2,2048,128]{2,1,0:T(8,128)(2,1)S(1)} %get-tuple-element.30.image0.own0, bf16[2,2048,128]{2,1,0:T(8,128)(2,1)S(1)} %get-tuple-element.31.image1.own1, f32[2,2,128,128]{3,2,1,0:T(8,128)S(1)} %get-tuple-element.38.kept_ref, ...), custom_call_target="tpu_custom_call" | custom-call | flops 1000 | bytes 1000 | tf_op jit(solution)/shard_map/final/pallas_call | solution.py:342
  (10 shorter events, 0.1 us)
Async XLA Ops:
  0.0 17.5 %collective-permute-start = (bf16[2,2048,128]{2,1,0:T(8,128)(2,1)}, bf16[2,2048,128]{2,1,0:T(8,128)(2,1)S(1)}, u32[]{:S(2)}, u32[]{:S(2)}) collective-permute-start(bf16[2,2048,128]{2,1,0:T(8,128)(2,1)} %bitcast.15), channel_id=1, source_target_pairs={{0,16},{16,32},{32,48},{48,64},{64,80},{80,96},{96,112},{112,128},... | collective-permute-start | bytes 3145736 | tf_op jit(solution)/shard_map/ppermute | solution.py:366
  1.9 28.6 %collective-permute-start.1 = (bf16[2,2048,128]{2,1,0:T(8,128)(2,1)}, bf16[2,2048,128]{2,1,0:T(8,128)(2,1)S(1)}, u32[]{:S(2)}, u32[]{:S(2)}) collective-permute-start(bf16[2,2048,128]{2,1,0:T(8,128)(2,1)} %bitcast.13), channel_id=1, source_target_pairs={{0,1},{1,2},{2,3},{3,4},{4,5},{5,6},{6,7},{7,8},{8,9},{9,10},{10,1... | collective-permute-start | bytes 3145736 | tf_op jit(solution)/shard_map/ppermute | solution.py:367
  17.5 1.2 copy-start
  33.2 12.5 %collective-permute-start.10 = (bf16[2,2048,128]{2,1,0:T(8,128)(2,1)S(1)}, bf16[2,2048,128]{2,1,0:T(8,128)(2,1)S(1)}, u32[]{:S(2)}, u32[]{:S(2)}) collective-permute-start(bf16[2,2048,128]{2,1,0:T(8,128)(2,1)S(1)} %get-tuple-element.31.image1.own1), channel_id=1, source_target_pairs={{6,5},{10,9},{14,13},{20,23},{24,27},{28,31},{38,37},{42,41},{46,4... | collective-permute-start | bytes 3145736 | tf_op jit(solution)/shard_map/ppermute | solution.py:389
  34.6 0.7 collective-permute-start.2
  35.9 0.7 collective-permute-start.3
  37.1 7.3 %collective-permute-start.4 = (f32[2,128,128]{2,1,0:T(8,128)S(1)}, f32[2,128,128]{2,1,0:T(8,128)S(1)}, u32[]{:S(2)}, u32[]{:S(2)}) collective-permute-start(f32[2,128,128]{2,1,0:T(8,128)S(1)} %get-tuple-element.36), channel_id=1, source_target_pairs={{2,3},{18,19},{34,35},{50,51},{66,67},{82,83},{98,99},{114,115},{1... | collective-permute-start | bytes 393224 | tf_op jit(solution)/shard_map/ppermute | solution.py:375
  37.8 10.0 %collective-permute-start.11 = (bf16[2,2048,128]{2,1,0:T(8,128)(2,1)S(1)}, bf16[2,2048,128]{2,1,0:T(8,128)(2,1)S(1)}, u32[]{:S(2)}, u32[]{:S(2)}) collective-permute-start(bf16[2,2048,128]{2,1,0:T(8,128)(2,1)S(1)} %get-tuple-element.31.image1.own1), channel_id=1, source_target_pairs={{7,5},{11,9},{15,13},{21,23},{25,27},{29,31},{39,37},{43,41},{47,4... | collective-permute-start | bytes 3145736 | tf_op jit(solution)/shard_map/ppermute | solution.py:389
  38.6 25.6 %collective-permute-start.12 = (bf16[2,2048,128]{2,1,0:T(8,128)(2,1)S(1)}, bf16[2,2048,128]{2,1,0:T(8,128)(2,1)S(1)}, u32[]{:S(2)}, u32[]{:S(2)}) collective-permute-start(bf16[2,2048,128]{2,1,0:T(8,128)(2,1)S(1)} %get-tuple-element.31.image1.own1), channel_id=1, source_target_pairs={{4,5},{8,9},{12,13},{22,23},{26,27},{30,31},{36,37},{40,41},{44,45... | collective-permute-start | bytes 3145736 | tf_op jit(solution)/shard_map/ppermute | solution.py:389
  43.2 21.7 %collective-permute-start.7 = (bf16[2,2048,128]{2,1,0:T(8,128)(2,1)S(1)}, bf16[2,2048,128]{2,1,0:T(8,128)(2,1)S(1)}, u32[]{:S(2)}, u32[]{:S(2)}) collective-permute-start(bf16[2,2048,128]{2,1,0:T(8,128)(2,1)S(1)} %get-tuple-element.30.image0.own0), channel_id=1, source_target_pairs={{5,4},{9,8},{13,12},{23,22},{27,26},{31,30},{37,36},{41,40},{45,44... | collective-permute-start | bytes 3145736 | tf_op jit(solution)/shard_map/ppermute | solution.py:389
  44.5 22.1 %collective-permute-start.8 = (bf16[2,2048,128]{2,1,0:T(8,128)(2,1)S(1)}, bf16[2,2048,128]{2,1,0:T(8,128)(2,1)S(1)}, u32[]{:S(2)}, u32[]{:S(2)}) collective-permute-start(bf16[2,2048,128]{2,1,0:T(8,128)(2,1)S(1)} %get-tuple-element.30.image0.own0), channel_id=1, source_target_pairs={{6,4},{10,8},{14,12},{20,22},{24,26},{28,30},{38,36},{42,40},{46,4... | collective-permute-start | bytes 3145736 | tf_op jit(solution)/shard_map/ppermute | solution.py:389
  45.8 28.7 %collective-permute-start.9 = (bf16[2,2048,128]{2,1,0:T(8,128)(2,1)S(1)}, bf16[2,2048,128]{2,1,0:T(8,128)(2,1)S(1)}, u32[]{:S(2)}, u32[]{:S(2)}) collective-permute-start(bf16[2,2048,128]{2,1,0:T(8,128)(2,1)S(1)} %get-tuple-element.30.image0.own0), channel_id=1, source_target_pairs={{7,4},{11,8},{15,12},{21,22},{25,26},{29,30},{39,36},{43,40},{47,4... | collective-permute-start | bytes 3145736 | tf_op jit(solution)/shard_map/ppermute | solution.py:389
  47.9 27.5 %collective-permute-start.5 = (f32[128,128]{1,0:T(8,128)S(1)}, f32[128,128]{1,0:T(8,128)S(1)}, u32[]{:S(2)}, u32[]{:S(2)}) collective-permute-start(f32[128,128]{1,0:T(8,128)S(1)} %get-tuple-element.39), channel_id=1, source_target_pairs={{3,4},{19,22},{35,36},{51,54},{67,68},{83,86},{99,100},{115,118},{... | collective-permute-start | bytes 196616 | tf_op jit(solution)/shard_map/ppermute | solution.py:377
  64.1 11.2 %collective-permute-start.6 = (f32[128,128]{1,0:T(8,128)S(1)}, f32[128,128]{1,0:T(8,128)S(1)}, u32[]{:S(2)}, u32[]{:S(2)}) collective-permute-start(f32[128,128]{1,0:T(8,128)S(1)} %get-tuple-element.40), channel_id=1, source_target_pairs={{3,5},{19,23},{35,37},{51,55},{67,69},{83,87},{99,101},{115,119},{... | collective-permute-start | bytes 196616 | tf_op jit(solution)/shard_map/ppermute | solution.py:377
  76.0 0.7 collective-permute-start.13
  77.3 16.5 %collective-permute-start.14 = (f32[128,128]{1,0:T(8,128)S(1)}, f32[128,128]{1,0:T(8,128)S(1)}, u32[]{:S(2)}, u32[]{:S(2)}) collective-permute-start(f32[128,128]{1,0:T(8,128)S(1)} %get-tuple-element.46), channel_id=1, source_target_pairs={{8,12},{9,13},{26,30},{27,31},{40,44},{41,45},{58,62},{59,63},{72,... | collective-permute-start | bytes 196616 | tf_op jit(solution)/shard_map/ppermute | solution.py:396
  98.6 8.2 %collective-permute-start.15 = (f32[2,128,128]{2,1,0:T(8,128)S(1)}, f32[2,128,128]{2,1,0:T(8,128)S(1)}, u32[]{:S(2)}, u32[]{:S(2)}) collective-permute-start(f32[2,128,128]{2,1,0:T(8,128)S(1)} %get-tuple-element.52), channel_id=1, source_target_pairs={{4,5},{8,9},{12,13},{22,23},{26,27},{30,31},{36,37},{40,41},{44,45... | collective-permute-start | bytes 393224 | tf_op jit(solution)/shard_map/ppermute | solution.py:397
  103.4 3.9 %collective-permute-start.16 = (f32[2,128,128]{2,1,0:T(8,128)S(1)}, f32[2,128,128]{2,1,0:T(8,128)S(1)}, u32[]{:S(2)}, u32[]{:S(2)}) collective-permute-start(f32[2,128,128]{2,1,0:T(8,128)S(1)} %get-tuple-element.53), channel_id=1, source_target_pairs={{4,6},{8,10},{12,14},{22,20},{26,24},{30,28},{36,38},{40,42},{44,4... | collective-permute-start | bytes 393224 | tf_op jit(solution)/shard_map/ppermute | solution.py:397
  104.7 6.9 %collective-permute-start.17 = (f32[2,128,128]{2,1,0:T(8,128)S(1)}, f32[2,128,128]{2,1,0:T(8,128)S(1)}, u32[]{:S(2)}, u32[]{:S(2)}) collective-permute-start(f32[2,128,128]{2,1,0:T(8,128)S(1)} %get-tuple-element.54), channel_id=1, source_target_pairs={{4,7},{8,11},{12,15},{22,21},{26,25},{30,29},{36,39},{40,43},{44,4... | collective-permute-start | bytes 393224 | tf_op jit(solution)/shard_map/ppermute | solution.py:397
